TPU v7x, 128 devices: a whole 4x4x4 slice. The times are simulated.
128 devices in a mesh: reg: 8 (over x, core), dam: 16 (over z, y).
Axes of the slice: x: 4, y: 4, z: 4, core: 2. Of those that a mesh axis runs over, the one named last changes fastest.
Arguments:
- history: bfloat16 [16384, 384], P(('reg', 'dam')), may hold values from -6 to 6
- routes: int32 [16384, 2], P(('reg', 'dam')), may hold values from 0 to 127, all different within a row; in each aligned block of 128 rows (0 to 127, 128 to 255, ...) at most 4 rows name the same one
- dam_field: bfloat16 [65536, 384], P(('reg', 'dam')), may hold values from -6 to 6
- conn_free: int32 [8192, 64], P(('reg', 'dam')), may hold values from 0 to 511
- conn_dam: int32 [8192, 64], P(('reg', 'dam')), may hold values from 0 to 511
- stiff_ref: bfloat16 [192, 192], replicated, may hold values from -0.4375 to 0.4375
- stiff_coef: float32 [8192], P(('reg', 'dam')), may hold values from 0.25 to 1
- mass_coef: float32 [8192], P(('reg', 'dam')), may hold values from 0.02 to 0.1
- reg_step: float32 [16384], P(('reg', 'dam')), may hold values from 0.05 to 0.2
- dam_step: float32 [65536], P(('reg', 'dam')), may hold values from 0.05 to 0.2
Outputs:
- history_out: bfloat16 [16384, 384], P(('reg', 'dam'))
- returned_force: float32 [16384, 384], P(('reg', 'dam'))
- dam_out: bfloat16 [65536, 384], P(('reg', 'dam'))
Inputs may be any that keep to these rules, and one draw needn't show every extreme that they name: `routes`: in the rows of one device no device number appears more than 4 times; some number appears exactly 4 times in some devices' rows.
All inputs are finite; a program needn't handle non-finite values.
Results may differ from a plain program's by a relative error of at most 0.0047.
Values may be sent and summed in bfloat16 or wider, within the bound.
A program may use at most 64 MiB of HBM per device.

v0:
```python
import jax
import jax.numpy as jnp
from jax import lax
from jax.experimental import pallas as pl
from jax.experimental.pallas import tpu as pltpu
from jax.sharding import PartitionSpec as P

ROUNDS = 2
GROUP = 4


def one_hot(indices, width):
    numbers = jnp.arange(width, dtype=jnp.int32)
    return (indices.reshape(-1)[:, None] == numbers[None, :]).astype(jnp.bfloat16)


def split_three(values):
    upper = lax.optimization_barrier(values.astype(jnp.bfloat16))
    rest = values - upper.astype(jnp.float32)
    middle = lax.optimization_barrier(rest.astype(jnp.bfloat16))
    lower = (rest - middle.astype(jnp.float32)).astype(jnp.bfloat16)
    return (upper, middle, lower)


def apply_exact(selector, values, transpose):
    dims = (((0,), (0,)), ((), ())) if transpose else (((1,), (0,)), ((), ()))
    total = None
    for piece in split_three(values):
        term = lax.dot_general(selector, piece, dims, preferred_element_type=jnp.float32)
        total = term if total is None else total + term
    return total


def block_places(routes, devices, capacity):
    entries = routes.reshape(-1)
    numbers = jnp.arange(devices, dtype=jnp.int32)
    onehot = (entries[:, None] == numbers[None, :]).astype(jnp.int32)
    before = jnp.cumsum(onehot, axis=0) - onehot
    slot = jnp.sum(before * onehot, axis=1)
    return entries * capacity + slot


def carry_blocks(outgoing, devices, capacity):
    row_width = outgoing.shape[1]
    shaped = outgoing.reshape(devices, capacity, row_width)
    arrived = lax.all_to_all(shaped, ("reg", "dam"), split_axis=0, concat_axis=0, tiled=True)
    return arrived.reshape(devices * capacity, row_width)


def element_kernel(sc_ref, mc_ref, r_ref, d_ref, cf_ref, cd_ref, s2_ref, dstep_ref,
                   back_ref, dnext_ref, dsum_ref):
    f32, bf16 = jnp.float32, jnp.bfloat16
    slots = r_ref.shape[0]
    dcount = d_ref.shape[0]
    groups, width = cf_ref.shape
    nodes = width // GROUP
    samples = r_ref.shape[1] // 3
    back_ref[...] = jnp.zeros(back_ref.shape, f32)
    dsum_ref[...] = jnp.zeros(dsum_ref.shape, f32)

    def body(g, carry):
        cf = cf_ref[pl.ds(g, 1), :]
        cd = cd_ref[pl.ds(g, 1), :]
        ohtf = (lax.broadcasted_iota(jnp.int32, (slots, width), 0) == cf).astype(f32)
        ohtd = (lax.broadcasted_iota(jnp.int32, (dcount, width), 0) == cd).astype(f32)
        ohf = jnp.transpose(ohtf).astype(bf16)
        ohd = jnp.transpose(ohtd).astype(bf16)
        uf = jnp.dot(ohf, r_ref[...], preferred_element_type=f32).astype(bf16)
        ud = jnp.dot(ohd, d_ref[...], preferred_element_type=f32).astype(bf16)
        forces = []
        for k in range(GROUP):
            e = g * GROUP + k
            lo_row, hi_row = k * nodes, (k + 1) * nodes
            wf = jnp.concatenate(
                [uf[lo_row:hi_row, c * samples:(c + 1) * samples] for c in range(3)], axis=0)
            wd = jnp.concatenate(
                [ud[lo_row:hi_row, c * samples:(c + 1) * samples] for c in range(3)], axis=0)
            x = jnp.concatenate([wf, wd], axis=0)
            ss = jnp.dot(s2_ref[...], x, preferred_element_type=f32)
            tot = wf.astype(f32) + wd.astype(f32)
            lane = lax.broadcasted_iota(jnp.int32, tot.shape, 1)
            prev = jnp.where(lane == 0, 0.0, pltpu.roll(tot, 1, 1))
            nxt = jnp.where(lane == samples - 1, 0.0, pltpu.roll(tot, samples - 1, 1))
            accel = (nxt - 2.0 * tot) + prev
            f = sc_ref[e] * ss + mc_ref[e] * accel
            forces.append(
                jnp.concatenate([f[c * nodes:(c + 1) * nodes, :] for c in range(3)], axis=1))
        fg = jnp.concatenate(forces, axis=0)
        hi = fg.astype(bf16)
        lo = (fg - hi.astype(f32)).astype(bf16)
        ohtf_b = ohtf.astype(bf16)
        ohtd_b = ohtd.astype(bf16)
        back_ref[...] += (jnp.dot(ohtf_b, hi, preferred_element_type=f32)
                          + jnp.dot(ohtf_b, lo, preferred_element_type=f32))
        dsum_ref[...] += (jnp.dot(ohtd_b, hi, preferred_element_type=f32)
                          + jnp.dot(ohtd_b, lo, preferred_element_type=f32))
        return carry

    lax.fori_loop(0, groups, body, 0)
    dnext_ref[...] = (d_ref[...].astype(f32) - dstep_ref[...] * dsum_ref[...]).astype(bf16)


def element_work(received, dam_field, conn_rows, dam_rows, s2, stiff_coef, mass_coef, dam_col):
    smem = pl.BlockSpec(memory_space=pltpu.SMEM)
    vmem = pl.BlockSpec(memory_space=pltpu.VMEM)
    return pl.pallas_call(
        element_kernel,
        out_shape=(jax.ShapeDtypeStruct(received.shape, jnp.float32),
                   jax.ShapeDtypeStruct(dam_field.shape, jnp.bfloat16)),
        in_specs=[smem, smem] + [vmem] * 6,
        out_specs=(vmem, vmem),
        scratch_shapes=[pltpu.VMEM(dam_field.shape, jnp.float32)],
    )(stiff_coef, mass_coef, received, dam_field, conn_rows, dam_rows, s2, dam_col)


def shards(history, routes, dam_field, conn_free, conn_dam, stiff_ref, stiff_coef,
           mass_coef, reg_step, dam_step):
    devices = lax.axis_size(("reg", "dam"))
    row_count, row_width = history.shape
    capacity = 4 * row_count // devices
    nodes = conn_free.shape[1]
    order = jnp.arange(3 * nodes)
    perm = (order % nodes) * 3 + order // nodes
    s_perm = stiff_ref[perm][:, perm]
    s2 = jnp.concatenate([s_perm, s_perm], axis=1)
    conn_rows = conn_free.reshape(-1, GROUP * nodes)
    dam_rows = conn_dam.reshape(-1, GROUP * nodes)
    dam_col = dam_step.reshape(-1, 1)
    places = block_places(routes, devices, capacity)
    place_select = one_hot(places, devices * capacity)
    pair_select = place_select.reshape(row_count, 2, devices * capacity).sum(axis=1)
    pulled = jnp.zeros((row_count, row_width), jnp.float32)
    for round_index in range(ROUNDS):
        spread = jnp.repeat(history, 2, axis=0)
        outgoing = lax.dot_general(
            place_select, spread, (((0,), (0,)), ((), ())), preferred_element_type=jnp.float32
        ).astype(jnp.bfloat16)
        received = carry_blocks(outgoing, devices, capacity)
        backward_sums, dam_field = element_work(
            received, dam_field, conn_rows, dam_rows, s2, stiff_coef, mass_coef, dam_col)
        returned = carry_blocks(backward_sums, devices, capacity)
        pulled = apply_exact(pair_select, returned, False)
        history = (history.astype(jnp.float32) - reg_step[:, None] * pulled).astype(jnp.bfloat16)
    return (history, pulled, dam_field)


def solution(mesh):
    in_specs = (
        P(("reg", "dam"), None),
        P(("reg", "dam"), None),
        P(("reg", "dam"), None),
        P(("reg", "dam"), None),
        P(("reg", "dam"), None),
        P(),
        P(("reg", "dam")),
        P(("reg", "dam")),
        P(("reg", "dam")),
        P(("reg", "dam")),
    )
    out_specs = (P(("reg", "dam"), None), P(("reg", "dam"), None), P(("reg", "dam"), None))
    return jax.shard_map(shards, mesh=mesh, in_specs=in_specs, out_specs=out_specs, check_vma=False)
```

profile of v0, /device:TPU:1, one launch (start us, length us, event | category | flops | bytes accessed | tf_op | source)
XLA Modules:
  0.0 146.8 jit_solution(17945206189601924257)
XLA Ops:
  0.6 0.8 copy.37
  2.4 0.7 copy-done.1
  3.7 0.8 reshape.148
  4.5 11.5 %all-to-all-start = ((bf16[128,4,384]{2,1,0:T(4,128)(2,1)}), bf16[128,4,384]{2,1,0:T(4,128)(2,1)S(1)}, u32[]{:S(2)}, u32[]{:S(2)}) async-start(bf16[128,4,384]{2,1,0:T(4,128)(2,1)} %reshape.148), calls=%async_computation | async-start | bytes 786432 | tf_op jit(solution)/shard_map/all_to_all | solution.py:46
  16.1 0.7 reshape.150.cf_ref
  16.8 0.7 reshape.151.cd_ref
  17.5 1.0 gather_fusion
  18.6 1.0 gather_fusion.1
  19.8 0.6 copy-done.5
  20.3 0.9 copy.44.dstep_ref
  21.2 0.8 pad_maximum_fusion.s2_ref
  22.0 6.8 %all-to-all-done = bf16[128,4,384]{2,1,0:T(4,128)(2,1)S(1)} async-done(((bf16[128,4,384]{2,1,0:T(4,128)(2,1)}), bf16[128,4,384]{2,1,0:T(4,128)(2,1)S(1)}, u32[]{:S(2)}, u32[]{:S(2)}) %all-to-all-start) | async-done | bytes 393248 | tf_op jit(solution)/shard_map/all_to_all | solution.py:46
  28.8 0.8 reshape.149.r_ref
  29.6 25.5 %shard_map.121 = (f32[512,384]{1,0:T(8,128)}, bf16[512,384]{1,0:T(8,128)(2,1)}) custom-call(f32[64]{0:T(128)} %sc_ref.3, f32[64]{0:T(128)} %mc_ref.3, bf16[512,384]{1,0:T(8,128)(2,1)} %reshape.149.r_ref, bf16[512,384]{1,0:T(8,128)(2,1)} %d_ref.1, s32[16,256]{1,0:T(8,128)} %reshape.150.cf_ref, s32[16,256]{1,0:T(8,128)} %reshape.151.cd_ref, ...), custom_call_target="tpu_custom_call" | custom-call | tf_op jit(solution)/shard_map/pallas_call | solution.py:106
  55.1 2.3 %reshape.153 = f32[128,4,384]{2,1,0:T(4,128)} reshape(f32[512,384]{1,0:T(8,128)} %get-tuple-element.7) | data formatting | bytes 1572864 | tf_op jit(solution)/shard_map/reshape | solution.py:45
  57.4 4.0 %all-to-all-start.1 = ((f32[128,4,384]{2,1,0:T(4,128)}), f32[128,4,384]{2,1,0:T(4,128)S(1)}, u32[]{:S(2)}, u32[]{:S(2)}) async-start(f32[128,4,384]{2,1,0:T(4,128)} %reshape.153), calls=%async_computation.1 | async-start | bytes 1572864 | tf_op jit(solution)/shard_map/all_to_all | solution.py:46
  61.6 0.6 copy-done.4
  62.3 15.8 %all-to-all-done.1 = f32[128,4,384]{2,1,0:T(4,128)S(1)} async-done(((f32[128,4,384]{2,1,0:T(4,128)}), f32[128,4,384]{2,1,0:T(4,128)S(1)}, u32[]{:S(2)}, u32[]{:S(2)}) %all-to-all-start.1) | async-done | bytes 786464 | tf_op jit(solution)/shard_map/all_to_all | solution.py:46
  80.4 16.5 %all_to_all.20 = bf16[128,4,384]{2,1,0:T(4,128)(2,1)S(1)} all-to-all(bf16[128,4,384]{2,1,0:T(4,128)(2,1)S(1)} %reshape.156), channel_id=1, replica_groups=mesh['reg'=8,'dam'=16] {'reg','dam'}, dimensions={0} | all-to-all | bytes 786432 | tf_op jit(solution)/shard_map/all_to_all | solution.py:46
  96.9 0.8 reshape.157.r_ref
  97.7 25.5 %shard_map.122 = (f32[512,384]{1,0:T(8,128)}, bf16[512,384]{1,0:T(8,128)(2,1)}) custom-call(f32[64]{0:T(128)} %sc_ref.3, f32[64]{0:T(128)} %mc_ref.3, bf16[512,384]{1,0:T(8,128)(2,1)} %reshape.157.r_ref, bf16[512,384]{1,0:T(8,128)(2,1)} %get-tuple-element.8.d_ref, s32[16,256]{1,0:T(8,128)} %reshape.150.cf_ref, s32[16,256]{1,0:T(8,128)} %reshape.151.cd_ref, ...), custom_call_target="tpu_custom_call" | custom-call | tf_op jit(solution)/shard_map/pallas_call | solution.py:106
  123.2 1.4 reshape.158
  124.6 20.4 %all_to_all.21 = f32[128,4,384]{2,1,0:T(4,128)S(1)} all-to-all(f32[128,4,384]{2,1,0:T(4,128)S(1)} %reshape.158), channel_id=1, replica_groups=mesh['reg'=8,'dam'=16] {'reg','dam'}, dimensions={0} | all-to-all | bytes 1572864 | tf_op jit(solution)/shard_map/all_to_all | solution.py:46
  145.9 1.0 subtract_convert_fusion.4
  (49 shorter events, 5.2 us)
Async XLA Ops:
  0.6 16.9 %copy-start = (bf16[192,192]{1,0:T(8,128)(2,1)S(1)}, bf16[192,192]{1,0:T(8,128)(2,1)}, u32[]{:S(2)}) copy-start(bf16[192,192]{1,0:T(8,128)(2,1)} %param.15) | copy-start | bytes 221188
  2.2 0.9 copy-start.1
  4.5 11.5 %copy-start.2 = (s32[64,64]{1,0:T(8,128)S(1)}, s32[64,64]{1,0:T(8,128)}, u32[]{:S(2)}) copy-start(s32[64,64]{1,0:T(8,128)} %param.13) | copy-start | bytes 49156
  4.5 24.3 %all-to-all-start = ((bf16[128,4,384]{2,1,0:T(4,128)(2,1)}), bf16[128,4,384]{2,1,0:T(4,128)(2,1)S(1)}, u32[]{:S(2)}, u32[]{:S(2)}) async-start(bf16[128,4,384]{2,1,0:T(4,128)(2,1)} %reshape.148), calls=%async_computation | async-start | bytes 786432 | tf_op jit(solution)/shard_map/all_to_all | solution.py:46
  16.0 0.8 copy-start.3
  19.6 0.7 copy-start.5
  57.4 20.8 %all-to-all-start.1 = ((f32[128,4,384]{2,1,0:T(4,128)}), f32[128,4,384]{2,1,0:T(4,128)S(1)}, u32[]{:S(2)}, u32[]{:S(2)}) async-start(f32[128,4,384]{2,1,0:T(4,128)} %reshape.153), calls=%async_computation.1 | async-start | bytes 1572864 | tf_op jit(solution)/shard_map/all_to_all | solution.py:46
  61.5 0.7 copy-start.4
  78.8 0.7 copy-start.6
where the time goes:
time: 147 us
  Pallas kernels  50.9 us (35%)
  blocking collectives  36.9 us (25%)
  waiting for transfers between devices  22.7 us (15%)
  starting transfers between devices  15.5 us (11%)
  local copies, waits for them, and re-layouts  15.4 us (10%)
  matrix products  3 us (2%)
  other arithmetic  1.58 us (1%)
    pallas_call x2, Pallas kernels, element_work(): pl.pallas_call(element_kernel, out_shape=(jax.ShapeDtypeStruct(received.s...  50.9 us
    all_to_all x2, blocking collectives, carry_blocks(): lax.all_to_all(shaped, ('reg', 'dam'), split_axis=0, concat_axis=0, tiled...  36.9 us
    all_to_all x2, waiting for transfers between devices, carry_blocks(): lax.all_to_all(shaped, ('reg', 'dam'), split_axis=0, concat_axis=0, tiled...  22.7 us
    all_to_all x2, starting transfers between devices, carry_blocks(): lax.all_to_all(shaped, ('reg', 'dam'), split_axis=0, concat_axis=0, tiled...  15.5 us
    reshape x4, local copies, waits for them, and re-layouts, carry_blocks(): shaped = outgoing.reshape(devices, capacity, row_width)  4.55 us
    unnamed x16, local copies, waits for them, and re-layouts  3.21 us
  transfers between devices with their start and end apart: 2, of which 2 were waited for; matrix products, arithmetic and copies ran while one was open for 4% of the time, Pallas kernels for 0%

commit v1 on v0

--- a/solution.py
+++ b/solution.py
@@ -1,3 +1,5 @@
+import functools
+
 import jax
 import jax.numpy as jnp
 from jax import lax
@@ -40,10 +42,62 @@
     return entries * capacity + slot
 
 
+def exchange_kernel(n, ndam, x_ref, o_ref, send_sem, recv_sem, local_sem):
+    me = lax.axis_index("reg") * ndam + lax.axis_index("dam")
+    mesh_id = pl.DeviceIdType.MESH
+    barrier = pltpu.get_barrier_semaphore()
+
+    def greet(step, carry):
+        peer = lax.rem(me + step, n)
+        pl.semaphore_signal(barrier, 1, device_id=(peer // ndam, peer % ndam),
+                            device_id_type=mesh_id)
+        return carry
+
+    lax.fori_loop(1, n, greet, 0)
+    pl.semaphore_wait(barrier, n - 1)
+
+    def send(step, carry):
+        peer = lax.rem(me + step, n)
+        pltpu.make_async_remote_copy(
+            src_ref=x_ref.at[peer],
+            dst_ref=o_ref.at[me],
+            send_sem=send_sem,
+            recv_sem=recv_sem,
+            device_id=(peer // ndam, peer % ndam),
+            device_id_type=mesh_id,
+        ).start()
+        return carry
+
+    own = pltpu.make_async_copy(x_ref.at[me], o_ref.at[me], local_sem)
+    own.start()
+    lax.fori_loop(1, n, send, 0)
+    everything = pltpu.make_async_remote_copy(
+        src_ref=x_ref.at[pl.ds(0, n - 1)],
+        dst_ref=o_ref.at[pl.ds(0, n - 1)],
+        send_sem=send_sem,
+        recv_sem=recv_sem,
+        device_id=(me // ndam, me % ndam),
+        device_id_type=mesh_id,
+    )
+    everything.wait_send()
+    everything.wait_recv()
+    own.wait()
+
+
 def carry_blocks(outgoing, devices, capacity):
+    ndam = lax.axis_size("dam")
     row_width = outgoing.shape[1]
     shaped = outgoing.reshape(devices, capacity, row_width)
-    arrived = lax.all_to_all(shaped, ("reg", "dam"), split_axis=0, concat_axis=0, tiled=True)
+    anywhere = pl.BlockSpec(memory_space=pl.ANY)
+    kernel_id = 1 if outgoing.dtype == jnp.float32 else 0
+    arrived = pl.pallas_call(
+        functools.partial(exchange_kernel, devices, ndam),
+        out_shape=jax.ShapeDtypeStruct(shaped.shape, shaped.dtype),
+        in_specs=[anywhere],
+        out_specs=anywhere,
+        scratch_shapes=[pltpu.SemaphoreType.DMA] * 3,
+        compiler_params=pltpu.CompilerParams(collective_id=kernel_id, has_side_effects=True),
+    )(shaped)
     return arrived.reshape(devices * capacity, row_width)
 
 

time: 147 us -> 149 us (1.014)
  Pallas kernels: 50.9 us -> 123 us
  blocking collectives: 36.9 us -> 0 us
  waiting for transfers between devices: 22.7 us -> 0 us
  starting transfers between devices: 15.5 us -> 0 us
  local copies, waits for them, and re-layouts: 15.4 us -> 20.2 us
    pallas_call x0 -> x4, Pallas kernels: none -> 71.7 us  [carry_blocks(): pl.pallas_call(functools.partial(exchange_kernel, devices, ndam), out_sha...]
    all_to_all x2 -> x0, blocking collectives: 36.9 us -> none  [carry_blocks(): lax.all_to_all(shaped, ('reg', 'dam'), split_axis=0, concat_axis=0, tiled...]
    all_to_all x2 -> x0, waiting for transfers between devices: 22.7 us -> none  [carry_blocks(): lax.all_to_all(shaped, ('reg', 'dam'), split_axis=0, concat_axis=0, tiled...]
    all_to_all x2 -> x0, starting transfers between devices: 15.5 us -> none  [carry_blocks(): lax.all_to_all(shaped, ('reg', 'dam'), split_axis=0, concat_axis=0, tiled...]
    reshape x4, local copies, waits for them, and re-layouts: 2.21 us -> 6.49 us  [carry_blocks(): return arrived.reshape(devices * capacity, row_width)]
    unnamed x16 -> x14, local copies, waits for them, and re-layouts: 3.21 us -> 1.34 us
    reshape x4, local copies, waits for them, and re-layouts: 4.55 us -> 6.2 us  [carry_blocks(): shaped = outgoing.reshape(devices, capacity, row_width)]
  transfers between devices with their start and end apart: 2 -> 0, of which waited for: 2 -> 0; matrix products, arithmetic and copies ran while one was open for 4% -> 0% of each run, Pallas kernels for 0% -> 0%
where the time goes in v1:
time: 149 us; the launch traced here: 148 us
  Pallas kernels  123 us (83%)
  local copies, waits for them, and re-layouts  20.2 us (14%)
  matrix products  2.99 us (2%)
  other arithmetic  1.58 us (1%)
    pallas_call x4, Pallas kernels, carry_blocks(): pl.pallas_call(functools.partial(exchange_kernel, devices, ndam), out_sha...  71.7 us
    pallas_call x2, Pallas kernels, element_work(): pl.pallas_call(element_kernel, out_shape=(jax.ShapeDtypeStruct(received.s...  50.9 us
    reshape x4, local copies, waits for them, and re-layouts, carry_blocks(): return arrived.reshape(devices * capacity, row_width)  6.49 us
    reshape x4, local copies, waits for them, and re-layouts, carry_blocks(): shaped = outgoing.reshape(devices, capacity, row_width)  6.2 us

profile of v1, /device:TPU:1, one launch (start us, length us, event | category | flops | bytes accessed | tf_op | source)
XLA Modules:
  0.0 148.3 jit_solution(7106346634285852935)
XLA Ops:
  0.7 1.5 reshape.150.cf_ref
  2.2 0.7 reshape.151.cd_ref
  4.1 1.0 gather_fusion
  5.2 1.0 gather_fusion.1
  6.3 0.8 pad_maximum_fusion.s2_ref
  7.2 0.8 copy-done.1
  8.1 0.4 convolution_convert_fusion.1
  8.6 0.8 reshape.148.x_ref
  9.4 19.6 %shard_map.121 = bf16[128,4,384]{2,1,0:T(4,128)(2,1)} custom-call(bf16[128,4,384]{2,1,0:T(4,128)(2,1)} %reshape.148.x_ref), custom_call_target="tpu_custom_call" | custom-call | tf_op jit(solution)/shard_map/pallas_call | solution.py:93
  29.1 1.8 %reshape.149.r_ref = bf16[512,384]{1,0:T(8,128)(2,1)} reshape(bf16[128,4,384]{2,1,0:T(4,128)(2,1)} %shard_map.121) | data formatting | bytes 786432 | tf_op jit(solution)/shard_map/reshape | solution.py:101
  30.9 0.9 copy.44.dstep_ref
  31.8 25.5 %shard_map.122 = (f32[512,384]{1,0:T(8,128)}, bf16[512,384]{1,0:T(8,128)(2,1)}) custom-call(f32[64]{0:T(128)} %sc_ref.3, f32[64]{0:T(128)} %mc_ref.3, bf16[512,384]{1,0:T(8,128)(2,1)} %reshape.149.r_ref, bf16[512,384]{1,0:T(8,128)(2,1)} %d_ref.1, s32[16,256]{1,0:T(8,128)} %reshape.150.cf_ref, s32[16,256]{1,0:T(8,128)} %reshape.151.cd_ref, ...), custom_call_target="tpu_custom_call" | custom-call | tf_op jit(solution)/shard_map/pallas_call | solution.py:160
  57.2 2.3 %reshape.153.x_ref = f32[128,4,384]{2,1,0:T(4,128)} reshape(f32[512,384]{1,0:T(8,128)} %get-tuple-element.7) | data formatting | bytes 1572864 | tf_op jit(solution)/shard_map/reshape | solution.py:90
  59.5 18.2 %shard_map.123 = f32[128,4,384]{2,1,0:T(4,128)} custom-call(f32[128,4,384]{2,1,0:T(4,128)} %reshape.153.x_ref), custom_call_target="tpu_custom_call" | custom-call | tf_op jit(solution)/shard_map/pallas_call | solution.py:93
  77.7 1.4 reshape.154
  80.6 0.4 convolution_convert_fusion
  81.1 0.8 reshape.156.x_ref
  81.9 15.5 %shard_map.124 = bf16[128,4,384]{2,1,0:T(4,128)(2,1)} custom-call(bf16[128,4,384]{2,1,0:T(4,128)(2,1)} %reshape.156.x_ref), custom_call_target="tpu_custom_call" | custom-call | tf_op jit(solution)/shard_map/pallas_call | solution.py:93
  97.4 1.8 %reshape.157.r_ref = bf16[512,384]{1,0:T(8,128)(2,1)} reshape(bf16[128,4,384]{2,1,0:T(4,128)(2,1)} %shard_map.124) | data formatting | bytes 786432 | tf_op jit(solution)/shard_map/reshape | solution.py:101
  99.3 25.5 %shard_map.125 = (f32[512,384]{1,0:T(8,128)}, bf16[512,384]{1,0:T(8,128)(2,1)}) custom-call(f32[64]{0:T(128)} %sc_ref.3, f32[64]{0:T(128)} %mc_ref.3, bf16[512,384]{1,0:T(8,128)(2,1)} %reshape.157.r_ref, bf16[512,384]{1,0:T(8,128)(2,1)} %get-tuple-element.8.d_ref, s32[16,256]{1,0:T(8,128)} %reshape.150.cf_ref, s32[16,256]{1,0:T(8,128)} %reshape.151.cd_ref, ...), custom_call_target="tpu_custom_call" | custom-call | tf_op jit(solution)/shard_map/pallas_call | solution.py:160
  124.7 2.3 %reshape.158.x_ref = f32[128,4,384]{2,1,0:T(4,128)} reshape(f32[512,384]{1,0:T(8,128)} %get-tuple-element.9) | data formatting | bytes 1572864 | tf_op jit(solution)/shard_map/reshape | solution.py:90
  127.0 18.3 %shard_map.126 = f32[128,4,384]{2,1,0:T(4,128)} custom-call(f32[128,4,384]{2,1,0:T(4,128)} %reshape.158.x_ref), custom_call_target="tpu_custom_call" | custom-call | tf_op jit(solution)/shard_map/pallas_call | solution.py:93
  145.3 1.4 reshape.159
  147.4 1.0 subtract_convert_fusion.4
  (45 shorter events, 3.7 us)
Async XLA Ops:
  0.6 3.4 %copy-start = (bf16[192,192]{1,0:T(8,128)(2,1)S(1)}, bf16[192,192]{1,0:T(8,128)(2,1)}, u32[]{:S(2)}) copy-start(bf16[192,192]{1,0:T(8,128)(2,1)} %param.15) | copy-start | bytes 221188
  0.6 1.5 %copy-start.2 = (s32[64,64]{1,0:T(8,128)S(1)}, s32[64,64]{1,0:T(8,128)}, u32[]{:S(2)}) copy-start(s32[64,64]{1,0:T(8,128)} %param.14) | copy-start | bytes 49156
  2.2 0.7 copy-start.3
  7.1 0.9 copy-start.1
  29.0 1.9 %copy-start.4 = (f32[512]{0:T(512)S(1)}, f32[512]{0:T(512)}, u32[]{:S(2)}) copy-start(f32[512]{0:T(512)} %param.19) | copy-start | bytes 6148
  79.5 0.7 copy-start.5

commit v2 on v0

v2 whole, which is shorter than its diff:
```python
import functools

import jax
import jax.numpy as jnp
from jax import lax
from jax.experimental import pallas as pl
from jax.experimental.pallas import tpu as pltpu
from jax.sharding import PartitionSpec as P

ROUNDS = 2
GROUP = 4


def one_hot(indices, width):
    numbers = jnp.arange(width, dtype=jnp.int32)
    return (indices.reshape(-1)[:, None] == numbers[None, :]).astype(jnp.bfloat16)


def block_places(routes, devices, capacity):
    entries = routes.reshape(-1)
    numbers = jnp.arange(devices, dtype=jnp.int32)
    onehot = (entries[:, None] == numbers[None, :]).astype(jnp.int32)
    before = jnp.cumsum(onehot, axis=0) - onehot
    slot = jnp.sum(before * onehot, axis=1)
    return entries * capacity + slot


def coupling_kernel(n, ndam, sc_ref, mc_ref, hist_ref, dam_ref, cf_ref, cd_ref, sp_ref,
                    dstep_ref, rstep_ref, qt_ref, q_ref,
                    hist_out, pulled_out, dam_out,
                    land_f0, land_f1, land_b0, land_b1,
                    stage_f, stage_b, landv_f, landv_b,
                    recv, ud_buf, ssd_buf, hi_buf, lo_buf, back, dsum, ret, sems):
    f32, bf16 = jnp.float32, jnp.bfloat16
    mesh_id = pl.DeviceIdType.MESH
    me = lax.axis_index("reg") * ndam + lax.axis_index("dam")
    slots = recv.shape[0]
    dcount = dam_out.shape[0]
    groups, width = cf_ref.shape
    nodes = width // GROUP
    samples = recv.shape[1] // 3
    lands_f, lands_b = (land_f0, land_f1), (land_b0, land_b1)
    blocks = stage_f.shape

    barrier = pltpu.get_barrier_semaphore()

    def greet(step, carry):
        peer = lax.rem(me + step, n)
        pl.semaphore_signal(barrier, 1, device_id=(peer // ndam, peer % ndam),
                            device_id_type=mesh_id)
        return carry

    lax.fori_loop(1, n, greet, 0)
    pl.semaphore_wait(barrier, n - 1)

    def local_copy(src, dst):
        cp = pltpu.make_async_copy(src, dst, sems.at[0])
        cp.start()
        cp.wait()

    def start_exchange(stage, land, base):
        own = pltpu.make_async_copy(stage.at[me], land.at[me], sems.at[base + 2])
        own.start()

        def send(step, carry):
            peer = lax.rem(me + step, n)
            pltpu.make_async_remote_copy(
                src_ref=stage.at[peer],
                dst_ref=land.at[me],
                send_sem=sems.at[base],
                recv_sem=sems.at[base + 1],
                device_id=(peer // ndam, peer % ndam),
                device_id_type=mesh_id,
            ).start()
            return carry

        lax.fori_loop(1, n, send, 0)
        return own

    def finish_exchange(stage, land, base, own):
        everything = pltpu.make_async_remote_copy(
            src_ref=stage.at[pl.ds(0, n - 1)],
            dst_ref=land.at[pl.ds(0, n - 1)],
            send_sem=sems.at[base],
            recv_sem=sems.at[base + 1],
            device_id=(me // ndam, me % ndam),
            device_id_type=mesh_id,
        )
        everything.wait_send()
        everything.wait_recv()
        own.wait()

    def dam_select(g):
        cd = cd_ref[pl.ds(g, 1), :]
        return (lax.broadcasted_iota(jnp.int32, (dcount, width), 0) == cd).astype(f32)

    def free_select(g):
        cf = cf_ref[pl.ds(g, 1), :]
        return (lax.broadcasted_iota(jnp.int32, (slots, width), 0) == cf).astype(f32)

    def node_major(u, k):
        lo_row, hi_row = k * nodes, (k + 1) * nodes
        return jnp.concatenate(
            [u[lo_row:hi_row, c * samples:(c + 1) * samples] for c in range(3)], axis=0)

    def dam_side(g, carry):
        ohd = jnp.transpose(dam_select(g)).astype(bf16)
        ud = jnp.dot(ohd, dam_out[...], preferred_element_type=f32).astype(bf16)
        rows = pl.ds(pl.multiple_of(g * width, width), width)
        ud_buf[rows, :] = ud
        for k in range(GROUP):
            ssd_buf[g * GROUP + k] = jnp.dot(sp_ref[...], node_major(ud, k),
                                             preferred_element_type=f32)
        return carry

    def free_side(g, carry):
        ohtf = free_select(g)
        ohf = jnp.transpose(ohtf).astype(bf16)
        uf = jnp.dot(ohf, recv[...], preferred_element_type=f32).astype(bf16)
        rows = pl.ds(pl.multiple_of(g * width, width), width)
        ud = ud_buf[rows, :]
        forces = []
        for k in range(GROUP):
            e = g * GROUP + k
            wf = node_major(uf, k)
            wd = node_major(ud, k)
            ss = ssd_buf[e] + jnp.dot(sp_ref[...], wf, preferred_element_type=f32)
            tot = wf.astype(f32) + wd.astype(f32)
            lane = lax.broadcasted_iota(jnp.int32, tot.shape, 1)
            prev = jnp.where(lane == 0, 0.0, pltpu.roll(tot, 1, 1))
            nxt = jnp.where(lane == samples - 1, 0.0, pltpu.roll(tot, samples - 1, 1))
            accel = (nxt - 2.0 * tot) + prev
            f = sc_ref[e] * ss + mc_ref[e] * accel
            forces.append(
                jnp.concatenate([f[c * nodes:(c + 1) * nodes, :] for c in range(3)], axis=1))
        fg = jnp.concatenate(forces, axis=0)
        hi = fg.astype(bf16)
        lo = (fg - hi.astype(f32)).astype(bf16)
        hi_buf[rows, :] = hi
        lo_buf[rows, :] = lo
        sel = ohtf.astype(bf16)
        back[...] += (jnp.dot(sel, hi, preferred_element_type=f32)
                      + jnp.dot(sel, lo, preferred_element_type=f32))
        return carry

    def dam_scatter(g, carry):
        sel = dam_select(g).astype(bf16)
        rows = pl.ds(pl.multiple_of(g * width, width), width)
        dsum[...] += (jnp.dot(sel, hi_buf[rows, :], preferred_element_type=f32)
                      + jnp.dot(sel, lo_buf[rows, :], preferred_element_type=f32))
        return carry

    hist_out[...] = hist_ref[...]
    dam_out[...] = dam_ref[...]
    for r in range(ROUNDS):
        base_f, base_b = 1 + 6 * r, 4 + 6 * r
        outgoing = jnp.dot(qt_ref[...], hist_out[...], preferred_element_type=f32).astype(bf16)
        stage_f[...] = outgoing.reshape(blocks)
        own_f = start_exchange(stage_f, lands_f[r], base_f)
        lax.fori_loop(0, groups, dam_side, 0)
        finish_exchange(stage_f, lands_f[r], base_f, own_f)
        local_copy(lands_f[r], landv_f)
        recv[...] = landv_f[...].reshape(recv.shape)

        back[...] = jnp.zeros(back.shape, f32)
        lax.fori_loop(0, groups, free_side, 0)
        stage_b[...] = back[...].reshape(blocks)
        own_b = start_exchange(stage_b, lands_b[r], base_b)
        dsum[...] = jnp.zeros(dsum.shape, f32)
        lax.fori_loop(0, groups, dam_scatter, 0)
        dam_out[...] = (dam_out[...].astype(f32) - dstep_ref[...] * dsum[...]).astype(bf16)
        finish_exchange(stage_b, lands_b[r], base_b, own_b)
        local_copy(lands_b[r], landv_b)
        ret[...] = landv_b[...].reshape(ret.shape)

        returned = ret[...]
        ret_hi = returned.astype(bf16)
        ret_lo = (returned - ret_hi.astype(f32)).astype(bf16)
        pulled = (jnp.dot(q_ref[...], ret_hi, preferred_element_type=f32)
                  + jnp.dot(q_ref[...], ret_lo, preferred_element_type=f32))
        hist_out[...] = (hist_out[...].astype(f32) - rstep_ref[...] * pulled).astype(bf16)
        if r == ROUNDS - 1:
            pulled_out[...] = pulled


def shards(history, routes, dam_field, conn_free, conn_dam, stiff_ref, stiff_coef,
           mass_coef, reg_step, dam_step):
    devices = lax.axis_size(("reg", "dam"))
    ndam = lax.axis_size("dam")
    row_count, row_width = history.shape
    capacity = 4 * row_count // devices
    slots = devices * capacity
    nodes = conn_free.shape[1]
    samples = row_width // 3
    order = jnp.arange(3 * nodes)
    perm = (order % nodes) * 3 + order // nodes
    s_perm = stiff_ref[perm][:, perm]
    conn_rows = conn_free.reshape(-1, GROUP * nodes)
    dam_rows = conn_dam.reshape(-1, GROUP * nodes)
    places = block_places(routes, devices, capacity)
    pair_select = one_hot(places, slots).reshape(row_count, 2, slots).sum(axis=1)
    smem = pl.BlockSpec(memory_space=pltpu.SMEM)
    vmem = pl.BlockSpec(memory_space=pltpu.VMEM)
    anywhere = pl.BlockSpec(memory_space=pl.ANY)
    elements = conn_free.shape[0]
    hbm_f = jax.ShapeDtypeStruct((devices, capacity, row_width), jnp.bfloat16)
    hbm_b = jax.ShapeDtypeStruct((devices, capacity, row_width), jnp.float32)
    outs = pl.pallas_call(
        functools.partial(coupling_kernel, devices, ndam),
        out_shape=(
            jax.ShapeDtypeStruct(history.shape, jnp.bfloat16),
            jax.ShapeDtypeStruct(history.shape, jnp.float32),
            jax.ShapeDtypeStruct(dam_field.shape, jnp.bfloat16),
            hbm_f, hbm_f, hbm_b, hbm_b,
        ),
        in_specs=[smem, smem] + [vmem] * 9,
        out_specs=(vmem, vmem, vmem) + (anywhere,) * 4,
        scratch_shapes=[
            pltpu.VMEM(hbm_f.shape, jnp.bfloat16),
            pltpu.VMEM(hbm_b.shape, jnp.float32),
            pltpu.VMEM(hbm_f.shape, jnp.bfloat16),
            pltpu.VMEM(hbm_b.shape, jnp.float32),
            pltpu.VMEM((slots, row_width), jnp.bfloat16),
            pltpu.VMEM((elements * nodes, row_width), jnp.bfloat16),
            pltpu.VMEM((elements, 3 * nodes, samples), jnp.float32),
            pltpu.VMEM((elements * nodes, row_width), jnp.bfloat16),
            pltpu.VMEM((elements * nodes, row_width), jnp.bfloat16),
            pltpu.VMEM((slots, row_width), jnp.float32),
            pltpu.VMEM(dam_field.shape, jnp.float32),
            pltpu.VMEM((slots, row_width), jnp.float32),
            pltpu.SemaphoreType.DMA((1 + 6 * ROUNDS,)),
        ],
        compiler_params=pltpu.CompilerParams(
            collective_id=0, has_side_effects=True, vmem_limit_bytes=48 * 1024 * 1024),
    )(stiff_coef, mass_coef, history, dam_field, conn_rows, dam_rows, s_perm,
      dam_step.reshape(-1, 1), reg_step.reshape(-1, 1), jnp.transpose(pair_select), pair_select)
    return (outs[0], outs[1], outs[2])


def solution(mesh):
    in_specs = (
        P(("reg", "dam"), None),
        P(("reg", "dam"), None),
        P(("reg", "dam"), None),
        P(("reg", "dam"), None),
        P(("reg", "dam"), None),
        P(),
        P(("reg", "dam")),
        P(("reg", "dam")),
        P(("reg", "dam")),
        P(("reg", "dam")),
    )
    out_specs = (P(("reg", "dam"), None), P(("reg", "dam"), None), P(("reg", "dam"), None))
    return jax.shard_map(shards, mesh=mesh, in_specs=in_specs, out_specs=out_specs, check_vma=False)
```

time: 147 us -> 111 us (0.76)
  Pallas kernels: 50.9 us -> 99.9 us
  blocking collectives: 36.9 us -> 0 us
  waiting for transfers between devices: 22.7 us -> 0 us
  starting transfers between devices: 15.5 us -> 0 us
  local copies, waits for them, and re-layouts: 15.4 us -> 8.91 us
  matrix products: 3 us -> 0 us
    pallas_call x2 -> x1, Pallas kernels: 50.9 us -> 99.9 us  [shards(): pl.pallas_call(functools.partial(coupling_kernel, devices, ndam), out_sha...]
    all_to_all x2 -> x0, blocking collectives: 36.9 us -> none  [carry_blocks(): lax.all_to_all(shaped, ('reg', 'dam'), split_axis=0, concat_axis=0, tiled...]
    all_to_all x2 -> x0, waiting for transfers between devices: 22.7 us -> none  [carry_blocks(): lax.all_to_all(shaped, ('reg', 'dam'), split_axis=0, concat_axis=0, tiled...]
    all_to_all x2 -> x0, starting transfers between devices: 15.5 us -> none  [carry_blocks(): lax.all_to_all(shaped, ('reg', 'dam'), split_axis=0, concat_axis=0, tiled...]
    reshape x11 -> x2, local copies, waits for them, and re-layouts: 7.79 us -> 0.26 us  [the longest x1 0.14 us: shards(): dam_step.reshape(-1, 1)]
    dot_general x8 -> x0, matrix products: 3 us -> none  [the longest x6 2.15 us: apply_exact(): lax.dot_general(selector, piece, dims, preferred_element_type=jnp.float32)]
    unnamed x16 -> x23, local copies, waits for them, and re-layouts: 3.21 us -> 4.79 us
  transfers between devices with their start and end apart: 2 -> 0, of which waited for: 2 -> 0; matrix products, arithmetic and copies ran while one was open for 4% -> 0% of each run, Pallas kernels for 0% -> 0%
where the time goes in v2:
time: 111 us; the launch traced here: 110 us
  Pallas kernels  99.9 us (90%)
  local copies, waits for them, and re-layouts  8.91 us (8%)
    pallas_call x1, Pallas kernels, shards(): pl.pallas_call(functools.partial(coupling_kernel, devices, ndam), out_sha...  99.9 us
    unnamed x23, local copies, waits for them, and re-layouts  4.79 us

profile of v2, /device:TPU:1, one launch (start us, length us, event | category | flops | bytes accessed | tf_op | source)
XLA Modules:
  0.0 110.2 jit_solution(14547280621170346350)
XLA Ops:
  0.7 0.9 reshape.117.cf_ref
  1.6 0.6 copy-done.6
  2.2 0.1 copy.43
  2.3 0.1 eq.45
  2.5 0.1 eq.41
  2.6 0.1 copy.45
  2.7 0.2 fusion.2
  3.0 0.2 fusion.4
  3.2 0.1 reduce_sum.24
  3.4 0.7 copy-done.8
  4.1 0.1 copy.50.rstep_ref
  4.2 1.0 gather_fusion
  5.2 0.1 copy.41
  5.3 1.0 gather_fusion.1
  6.4 0.1 copy.42
  6.5 0.1 fusion.1.q_ref
  6.6 0.1 copy.48
  6.7 0.5 copy-done.7
  7.3 0.1 copy.49.dstep_ref
  7.4 0.7 copy-done.2
  8.2 99.9 %shard_map.121 = (bf16[128,384]{1,0:T(8,128)(2,1)S(1)}, f32[128,384]{1,0:T(8,128)S(1)}, bf16[512,384]{1,0:T(8,128)(2,1)S(1)}, bf16[128,4,384]{2,1,0:T(4,128)(2,1...) custom-call(f32[64]{0:T(128)S(1)} %copy-done.3, f32[64]{0:T(128)S(1)} %copy-done.4, ...), custom_call_target="tpu_custom_call" | custom-call | tf_op jit(solution)/shard_map/pallas_call | solution.py:208
  108.1 0.6 copy.54
  108.8 0.7 copy.55
  109.5 0.7 copy.56
  (25 shorter events, 0.3 us)
Async XLA Ops:
  0.6 3.6 %copy-start = (bf16[192,192]{1,0:T(8,128)(2,1)S(1)}, bf16[192,192]{1,0:T(8,128)(2,1)}, u32[]{:S(2)}) copy-start(bf16[192,192]{1,0:T(8,128)(2,1)} %param.15) | copy-start | bytes 221188
  0.6 0.9 copy-start.5
  1.5 0.7 copy-start.6
  3.4 0.7 copy-start.8
  6.3 1.1 copy-start.1
  6.6 0.7 copy-start.7
  7.3 0.9 copy-start.2
  7.3 0.9 copy-start.3
  7.3 0.9 copy-start.4

commit v3 on v2

--- a/solution.py
+++ b/solution.py
@@ -30,7 +30,8 @@
                     hist_out, pulled_out, dam_out,
                     land_f0, land_f1, land_b0, land_b1,
                     stage_f, stage_b, landv_f, landv_b,
-                    recv, ud_buf, ssd_buf, hi_buf, lo_buf, back, dsum, ret, sems):
+                    recv, ud_buf, ssd_buf, hi_buf, lo_buf, back, dsum, ret,
+                    ohf_buf, ohd_buf, ohtf_buf, ohtd_buf, sems):
     f32, bf16 = jnp.float32, jnp.bfloat16
     mesh_id = pl.DeviceIdType.MESH
     me = lax.axis_index("reg") * ndam + lax.axis_index("dam")
@@ -51,6 +52,19 @@
         return carry
 
     lax.fori_loop(1, n, greet, 0)
+
+    def build_selectors(g, carry):
+        cf = cf_ref[pl.ds(g, 1), :]
+        cd = cd_ref[pl.ds(g, 1), :]
+        ohtf = (lax.broadcasted_iota(jnp.int32, (slots, width), 0) == cf).astype(f32)
+        ohtd = (lax.broadcasted_iota(jnp.int32, (dcount, width), 0) == cd).astype(f32)
+        ohtf_buf[g] = ohtf.astype(bf16)
+        ohtd_buf[g] = ohtd.astype(bf16)
+        ohf_buf[g] = jnp.transpose(ohtf).astype(bf16)
+        ohd_buf[g] = jnp.transpose(ohtd).astype(bf16)
+        return carry
+
+    lax.fori_loop(0, groups, build_selectors, 0)
     pl.semaphore_wait(barrier, n - 1)
 
     def local_copy(src, dst):
@@ -90,22 +104,13 @@
         everything.wait_recv()
         own.wait()
 
-    def dam_select(g):
-        cd = cd_ref[pl.ds(g, 1), :]
-        return (lax.broadcasted_iota(jnp.int32, (dcount, width), 0) == cd).astype(f32)
-
-    def free_select(g):
-        cf = cf_ref[pl.ds(g, 1), :]
-        return (lax.broadcasted_iota(jnp.int32, (slots, width), 0) == cf).astype(f32)
-
     def node_major(u, k):
         lo_row, hi_row = k * nodes, (k + 1) * nodes
         return jnp.concatenate(
             [u[lo_row:hi_row, c * samples:(c + 1) * samples] for c in range(3)], axis=0)
 
     def dam_side(g, carry):
-        ohd = jnp.transpose(dam_select(g)).astype(bf16)
-        ud = jnp.dot(ohd, dam_out[...], preferred_element_type=f32).astype(bf16)
+        ud = jnp.dot(ohd_buf[g], dam_out[...], preferred_element_type=f32).astype(bf16)
         rows = pl.ds(pl.multiple_of(g * width, width), width)
         ud_buf[rows, :] = ud
         for k in range(GROUP):
@@ -114,9 +119,7 @@
         return carry
 
     def free_side(g, carry):
-        ohtf = free_select(g)
-        ohf = jnp.transpose(ohtf).astype(bf16)
-        uf = jnp.dot(ohf, recv[...], preferred_element_type=f32).astype(bf16)
+        uf = jnp.dot(ohf_buf[g], recv[...], preferred_element_type=f32).astype(bf16)
         rows = pl.ds(pl.multiple_of(g * width, width), width)
         ud = ud_buf[rows, :]
         forces = []
@@ -138,16 +141,16 @@
         lo = (fg - hi.astype(f32)).astype(bf16)
         hi_buf[rows, :] = hi
         lo_buf[rows, :] = lo
-        sel = ohtf.astype(bf16)
-        back[...] += (jnp.dot(sel, hi, preferred_element_type=f32)
-                      + jnp.dot(sel, lo, preferred_element_type=f32))
+        both = jnp.dot(ohtf_buf[g], jnp.concatenate([hi, lo], axis=1),
+                       preferred_element_type=f32)
+        back[...] += both[:, :3 * samples] + both[:, 3 * samples:]
         return carry
 
     def dam_scatter(g, carry):
-        sel = dam_select(g).astype(bf16)
         rows = pl.ds(pl.multiple_of(g * width, width), width)
-        dsum[...] += (jnp.dot(sel, hi_buf[rows, :], preferred_element_type=f32)
-                      + jnp.dot(sel, lo_buf[rows, :], preferred_element_type=f32))
+        both = jnp.dot(ohtd_buf[g], jnp.concatenate([hi_buf[rows, :], lo_buf[rows, :]], axis=1),
+                       preferred_element_type=f32)
+        dsum[...] += both[:, :3 * samples] + both[:, 3 * samples:]
         return carry
 
     hist_out[...] = hist_ref[...]
@@ -203,6 +206,7 @@
     vmem = pl.BlockSpec(memory_space=pltpu.VMEM)
     anywhere = pl.BlockSpec(memory_space=pl.ANY)
     elements = conn_free.shape[0]
+    groups = conn_rows.shape[0]
     hbm_f = jax.ShapeDtypeStruct((devices, capacity, row_width), jnp.bfloat16)
     hbm_b = jax.ShapeDtypeStruct((devices, capacity, row_width), jnp.float32)
     outs = pl.pallas_call(
@@ -228,10 +232,14 @@
             pltpu.VMEM((slots, row_width), jnp.float32),
             pltpu.VMEM(dam_field.shape, jnp.float32),
             pltpu.VMEM((slots, row_width), jnp.float32),
+            pltpu.VMEM((groups, GROUP * nodes, slots), jnp.bfloat16),
+            pltpu.VMEM((groups, GROUP * nodes, dam_field.shape[0]), jnp.bfloat16),
+            pltpu.VMEM((groups, slots, GROUP * nodes), jnp.bfloat16),
+            pltpu.VMEM((groups, dam_field.shape[0], GROUP * nodes), jnp.bfloat16),
             pltpu.SemaphoreType.DMA((1 + 6 * ROUNDS,)),
         ],
         compiler_params=pltpu.CompilerParams(
-            collective_id=0, has_side_effects=True, vmem_limit_bytes=48 * 1024 * 1024),
+            collective_id=0, has_side_effects=True, vmem_limit_bytes=60 * 1024 * 1024),
     )(stiff_coef, mass_coef, history, dam_field, conn_rows, dam_rows, s_perm,
       dam_step.reshape(-1, 1), reg_step.reshape(-1, 1), jnp.transpose(pair_select), pair_select)
     return (outs[0], outs[1], outs[2])

time: 111 us -> 109 us (0.982)
  Pallas kernels: 99.9 us -> 94.4 us
  local copies, waits for them, and re-layouts: 8.91 us -> 12.7 us
    pallas_call x1, Pallas kernels: 99.9 us -> 94.4 us  [shards(): pl.pallas_call(functools.partial(coupling_kernel, devices, ndam), out_sha...]
    unnamed x23 -> x19, local copies, waits for them, and re-layouts: 4.79 us -> 4.78 us
where the time goes in v3:
time: 109 us; the launch traced here: 108 us
  Pallas kernels  94.4 us (87%)
  local copies, waits for them, and re-layouts  12.7 us (12%)
    pallas_call x1, Pallas kernels, shards(): pl.pallas_call(functools.partial(coupling_kernel, devices, ndam), out_sha...  94.4 us
    unnamed x19, local copies, waits for them, and re-layouts  4.78 us
    gather x4, local copies, waits for them, and re-layouts, shards(): s_perm = stiff_ref[perm][:, perm]  2.85 us

profile of v3, /device:TPU:1, one launch (start us, length us, event | category | flops | bytes accessed | tf_op | source)
XLA Modules:
  0.0 108.5 jit_solution(17628085383512798462)
XLA Ops:
  0.6 0.0 copy-start
  0.7 1.5 %reshape.117.cf_ref = s32[16,256]{1,0:T(8,128)} reshape(s32[64,64]{1,0:T(8,128)} %param.13) | data formatting | bytes 32768 | tf_op jit(solution)/shard_map/reshape | solution.py:201
  2.1 0.7 reshape.118.cd_ref
  2.8 0.1 copy.43
  2.9 0.1 eq.45
  3.1 0.1 eq.41
  3.2 0.1 copy.45
  3.3 0.2 fusion.2
  3.6 0.2 fusion.4
  3.8 0.1 reduce_sum.24
  4.0 0.1 copy.47
  4.0 0.7 copy-done.6
  4.7 0.7 copy.50.rstep_ref
  5.4 1.0 gather_fusion
  6.4 0.1 copy.41
  6.5 1.0 gather_fusion.1
  7.6 0.7 copy.42
  8.3 0.1 fusion.1.q_ref
  8.4 0.8 copy.48
  9.2 0.9 copy.49.dstep_ref
  10.1 94.4 %shard_map.121 = (bf16[128,384]{1,0:T(8,128)(2,1)}, f32[128,384]{1,0:T(8,128)}, bf16[512,384]{1,0:T(8,128)(2,1)}, bf16[128,4,384]{2,1,0:T(4,128)(2,1)}, bf16[128...) custom-call(f32[64]{0:T(128)} %sc_ref.1, f32[64]{0:T(128)} %mc_ref.1, ...), custom_call_target="tpu_custom_call" | custom-call | tf_op jit(solution)/shard_map/pallas_call | solution.py:212
  104.5 1.6 %copy.54 = bf16[128,384]{1,0:T(8,128)(2,1)} copy(bf16[128,384]{1,0:T(8,128)(2,1)} %get-tuple-element.12) | data formatting | bytes 196608
  106.1 1.6 %copy.55 = f32[128,384]{1,0:T(8,128)} copy(f32[128,384]{1,0:T(8,128)} %get-tuple-element.13) | data formatting | bytes 393216
  107.7 0.7 copy.56
  (21 shorter events, 0.1 us)
Async XLA Ops:
  0.6 4.8 %copy-start = (bf16[192,192]{1,0:T(8,128)(2,1)S(1)}, bf16[192,192]{1,0:T(8,128)(2,1)}, u32[]{:S(2)}) copy-start(bf16[192,192]{1,0:T(8,128)(2,1)} %param.15) | copy-start | bytes 221188
  0.6 1.5 %copy-start.3 = (s32[64,64]{1,0:T(8,128)S(1)}, s32[64,64]{1,0:T(8,128)}, u32[]{:S(2)}) copy-start(s32[64,64]{1,0:T(8,128)} %param.14) | copy-start | bytes 49156
  2.1 0.7 copy-start.4
  4.0 0.7 copy-start.6
  8.4 0.8 copy-start.1
  8.4 0.8 copy-start.5
  104.5 3.2 %copy-start.2 = (bf16[512,384]{1,0:T(8,128)(2,1)S(1)}, bf16[512,384]{1,0:T(8,128)(2,1)}, u32[]{:S(2)}) copy-start(bf16[512,384]{1,0:T(8,128)(2,1)} %get-tuple-element.14) | copy-start | bytes 1179652

commit v4 on v3

--- a/solution.py
+++ b/solution.py
@@ -25,20 +25,22 @@
     return entries * capacity + slot
 
 
-def coupling_kernel(n, ndam, sc_ref, mc_ref, hist_ref, dam_ref, cf_ref, cd_ref, sp_ref,
-                    dstep_ref, rstep_ref, qt_ref, q_ref,
+def coupling_kernel(n, ndam, sc_ref, mc_ref, hist_ref, dam_ref, cf_ref, cd_ref, stiff_ref,
+                    dstep_row, rstep_row, q_ref,
                     hist_out, pulled_out, dam_out,
                     land_f0, land_f1, land_b0, land_b1,
                     stage_f, stage_b, landv_f, landv_b,
                     recv, ud_buf, ssd_buf, hi_buf, lo_buf, back, dsum, ret,
-                    ohf_buf, ohd_buf, ohtf_buf, ohtd_buf, sems):
+                    ohf_buf, ohd_buf, ohtf_buf, ohtd_buf, sp_ref, qt_ref, dstep_ref, rstep_ref,
+                    sems):
     f32, bf16 = jnp.float32, jnp.bfloat16
     mesh_id = pl.DeviceIdType.MESH
     me = lax.axis_index("reg") * ndam + lax.axis_index("dam")
     slots = recv.shape[0]
     dcount = dam_out.shape[0]
-    groups, width = cf_ref.shape
-    nodes = width // GROUP
+    nodes = cf_ref.shape[1]
+    width = GROUP * nodes
+    groups = cf_ref.shape[0] // GROUP
     samples = recv.shape[1] // 3
     lands_f, lands_b = (land_f0, land_f1), (land_b0, land_b1)
     blocks = stage_f.shape
@@ -54,17 +56,31 @@
     lax.fori_loop(1, n, greet, 0)
 
     def build_selectors(g, carry):
-        cf = cf_ref[pl.ds(g, 1), :]
-        cd = cd_ref[pl.ds(g, 1), :]
-        ohtf = (lax.broadcasted_iota(jnp.int32, (slots, width), 0) == cf).astype(f32)
-        ohtd = (lax.broadcasted_iota(jnp.int32, (dcount, width), 0) == cd).astype(f32)
-        ohtf_buf[g] = ohtf.astype(bf16)
-        ohtd_buf[g] = ohtd.astype(bf16)
-        ohf_buf[g] = jnp.transpose(ohtf).astype(bf16)
-        ohd_buf[g] = jnp.transpose(ohtd).astype(bf16)
+        for k in range(GROUP):
+            lanes = slice(k * nodes, (k + 1) * nodes)
+            cf = cf_ref[pl.ds(g * GROUP + k, 1), :]
+            cd = cd_ref[pl.ds(g * GROUP + k, 1), :]
+            ohtf_buf[g, :, lanes] = (
+                lax.broadcasted_iota(jnp.int32, (slots, nodes), 0) == cf).astype(bf16)
+            ohtd_buf[g, :, lanes] = (
+                lax.broadcasted_iota(jnp.int32, (dcount, nodes), 0) == cd).astype(bf16)
+        ohf_buf[g] = jnp.transpose(ohtf_buf[g].astype(f32)).astype(bf16)
+        ohd_buf[g] = jnp.transpose(ohtd_buf[g].astype(f32)).astype(bf16)
         return carry
 
     lax.fori_loop(0, groups, build_selectors, 0)
+    size = sp_ref.shape[0]
+    across = lax.broadcasted_iota(jnp.int32, (size, size), 0)
+    down = lax.broadcasted_iota(jnp.int32, (size, size), 1)
+    pick_rows = (down == (across % nodes) * 3 + across // nodes).astype(bf16)
+    pick_cols = (across == (down % nodes) * 3 + down // nodes).astype(bf16)
+    permuted = jnp.dot(pick_rows, stiff_ref[...], preferred_element_type=f32).astype(bf16)
+    sp_ref[...] = jnp.dot(permuted, pick_cols, preferred_element_type=f32).astype(bf16)
+    qt_ref[...] = jnp.transpose(q_ref[...].astype(f32)).astype(bf16)
+    dstep_ref[...] = jnp.transpose(
+        jnp.broadcast_to(dstep_row[...], (8, dstep_row.shape[1])))[:, 0:1]
+    rstep_ref[...] = jnp.transpose(
+        jnp.broadcast_to(rstep_row[...], (8, rstep_row.shape[1])))[:, 0:1]
     pl.semaphore_wait(barrier, n - 1)
 
     def local_copy(src, dst):
@@ -195,18 +211,13 @@
     slots = devices * capacity
     nodes = conn_free.shape[1]
     samples = row_width // 3
-    order = jnp.arange(3 * nodes)
-    perm = (order % nodes) * 3 + order // nodes
-    s_perm = stiff_ref[perm][:, perm]
-    conn_rows = conn_free.reshape(-1, GROUP * nodes)
-    dam_rows = conn_dam.reshape(-1, GROUP * nodes)
     places = block_places(routes, devices, capacity)
     pair_select = one_hot(places, slots).reshape(row_count, 2, slots).sum(axis=1)
     smem = pl.BlockSpec(memory_space=pltpu.SMEM)
     vmem = pl.BlockSpec(memory_space=pltpu.VMEM)
     anywhere = pl.BlockSpec(memory_space=pl.ANY)
     elements = conn_free.shape[0]
-    groups = conn_rows.shape[0]
+    groups = conn_free.shape[0] // GROUP
     hbm_f = jax.ShapeDtypeStruct((devices, capacity, row_width), jnp.bfloat16)
     hbm_b = jax.ShapeDtypeStruct((devices, capacity, row_width), jnp.float32)
     outs = pl.pallas_call(
@@ -217,7 +228,7 @@
             jax.ShapeDtypeStruct(dam_field.shape, jnp.bfloat16),
             hbm_f, hbm_f, hbm_b, hbm_b,
         ),
-        in_specs=[smem, smem] + [vmem] * 9,
+        in_specs=[smem, smem] + [vmem] * 8,
         out_specs=(vmem, vmem, vmem) + (anywhere,) * 4,
         scratch_shapes=[
             pltpu.VMEM(hbm_f.shape, jnp.bfloat16),
@@ -236,12 +247,16 @@
             pltpu.VMEM((groups, GROUP * nodes, dam_field.shape[0]), jnp.bfloat16),
             pltpu.VMEM((groups, slots, GROUP * nodes), jnp.bfloat16),
             pltpu.VMEM((groups, dam_field.shape[0], GROUP * nodes), jnp.bfloat16),
+            pltpu.VMEM(stiff_ref.shape, jnp.bfloat16),
+            pltpu.VMEM((slots, row_count), jnp.bfloat16),
+            pltpu.VMEM((dam_field.shape[0], 1), jnp.float32),
+            pltpu.VMEM((row_count, 1), jnp.float32),
             pltpu.SemaphoreType.DMA((1 + 6 * ROUNDS,)),
         ],
         compiler_params=pltpu.CompilerParams(
             collective_id=0, has_side_effects=True, vmem_limit_bytes=60 * 1024 * 1024),
-    )(stiff_coef, mass_coef, history, dam_field, conn_rows, dam_rows, s_perm,
-      dam_step.reshape(-1, 1), reg_step.reshape(-1, 1), jnp.transpose(pair_select), pair_select)
+    )(stiff_coef, mass_coef, history, dam_field, conn_free, conn_dam, stiff_ref,
+      dam_step.reshape(1, -1), reg_step.reshape(1, -1), pair_select)
     return (outs[0], outs[1], outs[2])
 
 

time: 109 us -> 106 us (0.972)
  local copies, waits for them, and re-layouts: 12.7 us -> 5.36 us
  Pallas kernels: 94.4 us -> 98.4 us
    pallas_call x1, Pallas kernels: 94.4 us -> 98.4 us  [shards(): pl.pallas_call(functools.partial(coupling_kernel, devices, ndam), out_sha...]
    reshape x4 -> x0, local copies, waits for them, and re-layouts: 3.71 us -> none  [the longest x1 1.45 us: shards(): conn_rows = conn_free.reshape(-1, GROUP * nodes)]
    gather x4 -> x0, local copies, waits for them, and re-layouts: 2.85 us -> none  [shards(): s_perm = stiff_ref[perm][:, perm]]
    unnamed x19 -> x9, local copies, waits for them, and re-layouts: 4.78 us -> 4.75 us
where the time goes in v4:
time: 106 us
  Pallas kernels  98.4 us (93%)
  local copies, waits for them, and re-layouts  5.36 us (5%)
  other arithmetic  1.24 us (1%)
    pallas_call x1, Pallas kernels, shards(): pl.pallas_call(functools.partial(coupling_kernel, devices, ndam), out_sha...  98.4 us
    unnamed x9, local copies, waits for them, and re-layouts  4.75 us

profile of v4, /device:TPU:1, one launch (start us, length us, event | category | flops | bytes accessed | tf_op | source)
XLA Modules:
  0.0 105.7 jit_solution(7825989579983770686)
XLA Ops:
  0.6 0.0 copy-start.1
  0.6 0.7 copy-done.1
  1.3 0.1 copy.27
  1.4 0.1 eq.43
  1.6 0.1 eq.39
  1.7 0.1 copy.29
  1.8 0.2 fusion.2
  2.1 0.2 fusion.4
  2.3 0.1 reduce_sum.24
  2.5 0.1 copy.31
  2.5 0.8 fusion.1.q_ref
  3.3 98.4 %shard_map.121 = (bf16[128,384]{1,0:T(8,128)(2,1)}, f32[128,384]{1,0:T(8,128)}, bf16[512,384]{1,0:T(8,128)(2,1)}, bf16[128,4,384]{2,1,0:T(4,128)(2,1)}, bf16[128...) custom-call(f32[64]{0:T(128)} %sc_ref.1, f32[64]{0:T(128)} %mc_ref.1, ...), custom_call_target="tpu_custom_call" | custom-call | tf_op jit(solution)/shard_map/pallas_call | solution.py:223
  101.7 0.0 copy-start
  101.7 1.6 %copy.35 = bf16[128,384]{1,0:T(8,128)(2,1)} copy(bf16[128,384]{1,0:T(8,128)(2,1)} %get-tuple-element.12) | data formatting | bytes 196608
  103.3 1.6 %copy.36 = f32[128,384]{1,0:T(8,128)} copy(f32[128,384]{1,0:T(8,128)} %get-tuple-element.13) | data formatting | bytes 393216
  104.9 0.0 copy-done
  104.9 0.7 copy.37
  (7 shorter events, 0.1 us)
Async XLA Ops:
  0.6 0.7 copy-start.1
  101.7 3.2 %copy-start = (bf16[512,384]{1,0:T(8,128)(2,1)S(1)}, bf16[512,384]{1,0:T(8,128)(2,1)}, u32[]{:S(2)}) copy-start(bf16[512,384]{1,0:T(8,128)(2,1)} %get-tuple-element.14) | copy-start | bytes 1179652

commit v5 on v4

--- a/solution.py
+++ b/solution.py
@@ -9,6 +9,7 @@
 
 ROUNDS = 2
 GROUP = 4
+GATHER_PARTS = 4
 
 
 def one_hot(indices, width):
@@ -31,7 +32,7 @@
                     land_f0, land_f1, land_b0, land_b1,
                     stage_f, stage_b, landv_f, landv_b,
                     recv, ud_buf, ssd_buf, hi_buf, lo_buf, back, dsum, ret,
-                    ohf_buf, ohd_buf, ohtf_buf, ohtd_buf, sp_ref, qt_ref, dstep_ref, rstep_ref,
+                    ohf_buf, ohd_buf, ohtf_buf, ohtd_buf, uf_buf, sp_ref, qt_ref, dstep_ref, rstep_ref,
                     sems):
     f32, bf16 = jnp.float32, jnp.bfloat16
     mesh_id = pl.DeviceIdType.MESH
@@ -64,8 +65,9 @@
                 lax.broadcasted_iota(jnp.int32, (slots, nodes), 0) == cf).astype(bf16)
             ohtd_buf[g, :, lanes] = (
                 lax.broadcasted_iota(jnp.int32, (dcount, nodes), 0) == cd).astype(bf16)
-        ohf_buf[g] = jnp.transpose(ohtf_buf[g].astype(f32)).astype(bf16)
-        ohd_buf[g] = jnp.transpose(ohtd_buf[g].astype(f32)).astype(bf16)
+        rows = pl.ds(pl.multiple_of(g * width, width), width)
+        ohf_buf[rows, :] = jnp.transpose(ohtf_buf[g].astype(f32)).astype(bf16)
+        ohd_buf[rows, :] = jnp.transpose(ohtd_buf[g].astype(f32)).astype(bf16)
         return carry
 
     lax.fori_loop(0, groups, build_selectors, 0)
@@ -125,18 +127,23 @@
         return jnp.concatenate(
             [u[lo_row:hi_row, c * samples:(c + 1) * samples] for c in range(3)], axis=0)
 
+    def gather_all(select, table, out):
+        for part in range(GATHER_PARTS):
+            rows = slice(part * out.shape[0] // GATHER_PARTS, (part + 1) * out.shape[0] // GATHER_PARTS)
+            out[rows, :] = jnp.dot(select[rows, :], table[...],
+                                   preferred_element_type=f32).astype(bf16)
+
     def dam_side(g, carry):
-        ud = jnp.dot(ohd_buf[g], dam_out[...], preferred_element_type=f32).astype(bf16)
-        rows = pl.ds(pl.multiple_of(g * width, width), width)
-        ud_buf[rows, :] = ud
+        rows = pl.ds(pl.multiple_of(g * width, width), width)
+        ud = ud_buf[rows, :]
         for k in range(GROUP):
             ssd_buf[g * GROUP + k] = jnp.dot(sp_ref[...], node_major(ud, k),
                                              preferred_element_type=f32)
         return carry
 
     def free_side(g, carry):
-        uf = jnp.dot(ohf_buf[g], recv[...], preferred_element_type=f32).astype(bf16)
-        rows = pl.ds(pl.multiple_of(g * width, width), width)
+        rows = pl.ds(pl.multiple_of(g * width, width), width)
+        uf = uf_buf[rows, :]
         ud = ud_buf[rows, :]
         forces = []
         for k in range(GROUP):
@@ -176,12 +183,14 @@
         outgoing = jnp.dot(qt_ref[...], hist_out[...], preferred_element_type=f32).astype(bf16)
         stage_f[...] = outgoing.reshape(blocks)
         own_f = start_exchange(stage_f, lands_f[r], base_f)
+        gather_all(ohd_buf, dam_out, ud_buf)
         lax.fori_loop(0, groups, dam_side, 0)
         finish_exchange(stage_f, lands_f[r], base_f, own_f)
         local_copy(lands_f[r], landv_f)
         recv[...] = landv_f[...].reshape(recv.shape)
 
         back[...] = jnp.zeros(back.shape, f32)
+        gather_all(ohf_buf, recv, uf_buf)
         lax.fori_loop(0, groups, free_side, 0)
         stage_b[...] = back[...].reshape(blocks)
         own_b = start_exchange(stage_b, lands_b[r], base_b)
@@ -243,10 +252,11 @@
             pltpu.VMEM((slots, row_width), jnp.float32),
             pltpu.VMEM(dam_field.shape, jnp.float32),
             pltpu.VMEM((slots, row_width), jnp.float32),
-            pltpu.VMEM((groups, GROUP * nodes, slots), jnp.bfloat16),
-            pltpu.VMEM((groups, GROUP * nodes, dam_field.shape[0]), jnp.bfloat16),
+            pltpu.VMEM((elements * nodes, slots), jnp.bfloat16),
+            pltpu.VMEM((elements * nodes, dam_field.shape[0]), jnp.bfloat16),
             pltpu.VMEM((groups, slots, GROUP * nodes), jnp.bfloat16),
             pltpu.VMEM((groups, dam_field.shape[0], GROUP * nodes), jnp.bfloat16),
+            pltpu.VMEM((elements * nodes, row_width), jnp.bfloat16),
             pltpu.VMEM(stiff_ref.shape, jnp.bfloat16),
             pltpu.VMEM((slots, row_count), jnp.bfloat16),
             pltpu.VMEM((dam_field.shape[0], 1), jnp.float32),

time: 106 us -> 100 us (0.943)
  Pallas kernels: 98.4 us -> 92.8 us
    pallas_call x1, Pallas kernels: 98.4 us -> 92.8 us  [shards(): pl.pallas_call(functools.partial(coupling_kernel, devices, ndam), out_sha...]
where the time goes in v5:
time: 100 us
  Pallas kernels  92.8 us (93%)
  local copies, waits for them, and re-layouts  5.36 us (5%)
  other arithmetic  1.24 us (1%)
    pallas_call x1, Pallas kernels, shards(): pl.pallas_call(functools.partial(coupling_kernel, devices, ndam), out_sha...  92.8 us
    unnamed x9, local copies, waits for them, and re-layouts  4.75 us

profile of v5, /device:TPU:1, one launch (start us, length us, event | category | flops | bytes accessed | tf_op | source)
XLA Modules:
  0.0 100.1 jit_solution(2110936843972682417)
XLA Ops:
  0.6 0.0 copy-start.1
  0.6 0.7 copy-done.1
  1.3 0.1 copy.27
  1.4 0.1 eq.43
  1.6 0.1 eq.39
  1.7 0.1 copy.29
  1.8 0.2 fusion.2
  2.1 0.2 fusion.4
  2.3 0.1 reduce_sum.24
  2.5 0.1 copy.31
  2.5 0.8 fusion.1.q_ref
  3.3 92.8 %shard_map.121 = (bf16[128,384]{1,0:T(8,128)(2,1)}, f32[128,384]{1,0:T(8,128)}, bf16[512,384]{1,0:T(8,128)(2,1)}, bf16[128,4,384]{2,1,0:T(4,128)(2,1)}, bf16[128...) custom-call(f32[64]{0:T(128)} %sc_ref.1, f32[64]{0:T(128)} %mc_ref.1, ...), custom_call_target="tpu_custom_call" | custom-call | tf_op jit(solution)/shard_map/pallas_call | solution.py:232
  96.2 0.0 copy-start
  96.2 1.6 %copy.35 = bf16[128,384]{1,0:T(8,128)(2,1)} copy(bf16[128,384]{1,0:T(8,128)(2,1)} %get-tuple-element.12) | data formatting | bytes 196608
  97.8 1.6 %copy.36 = f32[128,384]{1,0:T(8,128)} copy(f32[128,384]{1,0:T(8,128)} %get-tuple-element.13) | data formatting | bytes 393216
  99.4 0.0 copy-done
  99.4 0.7 copy.37
  (7 shorter events, 0.1 us)
Async XLA Ops:
  0.6 0.7 copy-start.1
  96.2 3.2 %copy-start = (bf16[512,384]{1,0:T(8,128)(2,1)S(1)}, bf16[512,384]{1,0:T(8,128)(2,1)}, u32[]{:S(2)}) copy-start(bf16[512,384]{1,0:T(8,128)(2,1)} %get-tuple-element.14) | copy-start | bytes 1179652

commit v6 on v5

--- a/solution.py
+++ b/solution.py
@@ -136,9 +136,8 @@
     def dam_side(g, carry):
         rows = pl.ds(pl.multiple_of(g * width, width), width)
         ud = ud_buf[rows, :]
-        for k in range(GROUP):
-            ssd_buf[g * GROUP + k] = jnp.dot(sp_ref[...], node_major(ud, k),
-                                             preferred_element_type=f32)
+        side = jnp.concatenate([node_major(ud, k) for k in range(GROUP)], axis=1)
+        ssd_buf[g] = jnp.dot(sp_ref[...], side, preferred_element_type=f32)
         return carry
 
     def free_side(g, carry):
@@ -146,11 +145,14 @@
         uf = uf_buf[rows, :]
         ud = ud_buf[rows, :]
         forces = []
+        free_all = [node_major(uf, k) for k in range(GROUP)]
+        ss_all = ssd_buf[g] + jnp.dot(sp_ref[...], jnp.concatenate(free_all, axis=1),
+                                      preferred_element_type=f32)
         for k in range(GROUP):
             e = g * GROUP + k
-            wf = node_major(uf, k)
+            wf = free_all[k]
             wd = node_major(ud, k)
-            ss = ssd_buf[e] + jnp.dot(sp_ref[...], wf, preferred_element_type=f32)
+            ss = ss_all[:, k * samples:(k + 1) * samples]
             tot = wf.astype(f32) + wd.astype(f32)
             lane = lax.broadcasted_iota(jnp.int32, tot.shape, 1)
             prev = jnp.where(lane == 0, 0.0, pltpu.roll(tot, 1, 1))
@@ -246,7 +248,7 @@
             pltpu.VMEM(hbm_b.shape, jnp.float32),
             pltpu.VMEM((slots, row_width), jnp.bfloat16),
             pltpu.VMEM((elements * nodes, row_width), jnp.bfloat16),
-            pltpu.VMEM((elements, 3 * nodes, samples), jnp.float32),
+            pltpu.VMEM((groups, 3 * nodes, GROUP * samples), jnp.float32),
             pltpu.VMEM((elements * nodes, row_width), jnp.bfloat16),
             pltpu.VMEM((elements * nodes, row_width), jnp.bfloat16),
             pltpu.VMEM((slots, row_width), jnp.float32),

time: 100 us -> 99.4 us (level)
  Pallas kernels: 92.8 us -> 91.7 us
    pallas_call x1, Pallas kernels: 92.8 us -> 91.7 us  [shards(): pl.pallas_call(functools.partial(coupling_kernel, devices, ndam), out_sha...]
where the time goes in v6:
time: 99.4 us; the launch traced here: 99 us
  Pallas kernels  91.7 us (92%)
  local copies, waits for them, and re-layouts  5.36 us (5%)
  other arithmetic  1.24 us (1%)
    pallas_call x1, Pallas kernels, shards(): pl.pallas_call(functools.partial(coupling_kernel, devices, ndam), out_sha...  91.7 us
    unnamed x9, local copies, waits for them, and re-layouts  4.75 us

profile of v6, /device:TPU:1, one launch (start us, length us, event | category | flops | bytes accessed | tf_op | source)
XLA Modules:
  0.0 99.0 jit_solution(16800287490707662791)
XLA Ops:
  0.6 0.0 copy-start.1
  0.6 0.7 copy-done.1
  1.3 0.1 copy.27
  1.4 0.1 eq.43
  1.6 0.1 eq.39
  1.7 0.1 copy.29
  1.8 0.2 fusion.2
  2.1 0.2 fusion.4
  2.3 0.1 reduce_sum.24
  2.5 0.1 copy.31
  2.5 0.8 fusion.1.q_ref
  3.3 91.7 %shard_map.121 = (bf16[128,384]{1,0:T(8,128)(2,1)}, f32[128,384]{1,0:T(8,128)}, bf16[512,384]{1,0:T(8,128)(2,1)}, bf16[128,4,384]{2,1,0:T(4,128)(2,1)}, bf16[128...) custom-call(f32[64]{0:T(128)} %sc_ref.1, f32[64]{0:T(128)} %mc_ref.1, ...), custom_call_target="tpu_custom_call" | custom-call | tf_op jit(solution)/shard_map/pallas_call | solution.py:234
  95.1 0.0 copy-start
  95.1 1.6 %copy.35 = bf16[128,384]{1,0:T(8,128)(2,1)} copy(bf16[128,384]{1,0:T(8,128)(2,1)} %get-tuple-element.12) | data formatting | bytes 196608
  96.7 1.6 %copy.36 = f32[128,384]{1,0:T(8,128)} copy(f32[128,384]{1,0:T(8,128)} %get-tuple-element.13) | data formatting | bytes 393216
  98.3 0.0 copy-done
  98.3 0.7 copy.37
  (7 shorter events, 0.1 us)
Async XLA Ops:
  0.6 0.7 copy-start.1
  95.1 3.2 %copy-start = (bf16[512,384]{1,0:T(8,128)(2,1)S(1)}, bf16[512,384]{1,0:T(8,128)(2,1)}, u32[]{:S(2)}) copy-start(bf16[512,384]{1,0:T(8,128)(2,1)} %get-tuple-element.14) | copy-start | bytes 1179652

commit v7 on v6

--- a/solution.py
+++ b/solution.py
@@ -12,27 +12,13 @@
 GATHER_PARTS = 4
 
 
-def one_hot(indices, width):
-    numbers = jnp.arange(width, dtype=jnp.int32)
-    return (indices.reshape(-1)[:, None] == numbers[None, :]).astype(jnp.bfloat16)
-
-
-def block_places(routes, devices, capacity):
-    entries = routes.reshape(-1)
-    numbers = jnp.arange(devices, dtype=jnp.int32)
-    onehot = (entries[:, None] == numbers[None, :]).astype(jnp.int32)
-    before = jnp.cumsum(onehot, axis=0) - onehot
-    slot = jnp.sum(before * onehot, axis=1)
-    return entries * capacity + slot
-
-
 def coupling_kernel(n, ndam, sc_ref, mc_ref, hist_ref, dam_ref, cf_ref, cd_ref, stiff_ref,
-                    dstep_row, rstep_row, q_ref,
+                    dstep_row, rstep_row, routes_ref,
                     hist_out, pulled_out, dam_out,
                     land_f0, land_f1, land_b0, land_b1,
                     stage_f, stage_b, landv_f, landv_b,
                     recv, ud_buf, ssd_buf, hi_buf, lo_buf, back, dsum, ret,
-                    ohf_buf, ohd_buf, ohtf_buf, ohtd_buf, uf_buf, sp_ref, qt_ref, dstep_ref, rstep_ref,
+                    ohf_buf, ohd_buf, ohtf_buf, ohtd_buf, uf_buf, sp_ref, q_ref, qt_ref, dstep_ref, rstep_ref,
                     sems):
     f32, bf16 = jnp.float32, jnp.bfloat16
     mesh_id = pl.DeviceIdType.MESH
@@ -78,7 +64,24 @@
     pick_cols = (across == (down % nodes) * 3 + down // nodes).astype(bf16)
     permuted = jnp.dot(pick_rows, stiff_ref[...], preferred_element_type=f32).astype(bf16)
     sp_ref[...] = jnp.dot(permuted, pick_cols, preferred_element_type=f32).astype(bf16)
-    qt_ref[...] = jnp.transpose(q_ref[...].astype(f32)).astype(bf16)
+    regional = routes_ref.shape[0]
+    capacity = slots // n
+    first = routes_ref[:, 0:1]
+    second = routes_ref[:, 1:2]
+    numbers = lax.broadcasted_iota(jnp.int32, (regional, n), 1)
+    hit_first = (first == numbers).astype(f32)
+    hit_second = (second == numbers).astype(f32)
+    earlier = (lax.broadcasted_iota(jnp.int32, (regional, regional), 1)
+               < lax.broadcasted_iota(jnp.int32, (regional, regional), 0)).astype(bf16)
+    counts = jnp.dot(earlier, (hit_first + hit_second).astype(bf16), preferred_element_type=f32)
+    slot_first = jnp.sum(counts * hit_first, axis=1, keepdims=True).astype(jnp.int32)
+    slot_second = jnp.sum(counts * hit_second, axis=1, keepdims=True).astype(jnp.int32)
+    place_first = first * capacity + slot_first
+    place_second = second * capacity + slot_second
+    columns = lax.broadcasted_iota(jnp.int32, (regional, slots), 1)
+    pair = jnp.logical_or(columns == place_first, columns == place_second).astype(f32)
+    q_ref[...] = pair.astype(bf16)
+    qt_ref[...] = jnp.transpose(pair).astype(bf16)
     dstep_ref[...] = jnp.transpose(
         jnp.broadcast_to(dstep_row[...], (8, dstep_row.shape[1])))[:, 0:1]
     rstep_ref[...] = jnp.transpose(
@@ -222,8 +225,6 @@
     slots = devices * capacity
     nodes = conn_free.shape[1]
     samples = row_width // 3
-    places = block_places(routes, devices, capacity)
-    pair_select = one_hot(places, slots).reshape(row_count, 2, slots).sum(axis=1)
     smem = pl.BlockSpec(memory_space=pltpu.SMEM)
     vmem = pl.BlockSpec(memory_space=pltpu.VMEM)
     anywhere = pl.BlockSpec(memory_space=pl.ANY)
@@ -260,6 +261,7 @@
             pltpu.VMEM((groups, dam_field.shape[0], GROUP * nodes), jnp.bfloat16),
             pltpu.VMEM((elements * nodes, row_width), jnp.bfloat16),
             pltpu.VMEM(stiff_ref.shape, jnp.bfloat16),
+            pltpu.VMEM((row_count, slots), jnp.bfloat16),
             pltpu.VMEM((slots, row_count), jnp.bfloat16),
             pltpu.VMEM((dam_field.shape[0], 1), jnp.float32),
             pltpu.VMEM((row_count, 1), jnp.float32),
@@ -268,7 +270,7 @@
         compiler_params=pltpu.CompilerParams(
             collective_id=0, has_side_effects=True, vmem_limit_bytes=60 * 1024 * 1024),
     )(stiff_coef, mass_coef, history, dam_field, conn_free, conn_dam, stiff_ref,
-      dam_step.reshape(1, -1), reg_step.reshape(1, -1), pair_select)
+      dam_step.reshape(1, -1), reg_step.reshape(1, -1), routes)
     return (outs[0], outs[1], outs[2])
 
 

time: 99.4 us -> 98.4 us (0.990)
  other arithmetic: 1.24 us -> 0 us
    unnamed x9 -> x8, local copies, waits for them, and re-layouts: 4.75 us -> 5.37 us
where the time goes in v7:
time: 98.4 us; the launch traced here: 98 us
  Pallas kernels  92 us (93%)
  local copies, waits for them, and re-layouts  5.37 us (5%)
    pallas_call x1, Pallas kernels, shards(): pl.pallas_call(functools.partial(coupling_kernel, devices, ndam), out_sha...  92 us
    unnamed x8, local copies, waits for them, and re-layouts  5.37 us

profile of v7, /device:TPU:1, one launch (start us, length us, event | category | flops | bytes accessed | tf_op | source)
XLA Modules:
  0.0 98.0 jit_solution(1277451284501286580)
XLA Ops:
  0.6 0.0 copy-start.1
  0.6 0.7 copy-done.1
  1.3 0.7 copy.13.routes_ref
  2.1 92.0 %shard_map.121 = (bf16[128,384]{1,0:T(8,128)(2,1)}, f32[128,384]{1,0:T(8,128)}, bf16[512,384]{1,0:T(8,128)(2,1)}, bf16[128,4,384]{2,1,0:T(4,128)(2,1)}, bf16[128...) custom-call(f32[64]{0:T(128)} %sc_ref.1, f32[64]{0:T(128)} %mc_ref.1, ...), custom_call_target="tpu_custom_call" | custom-call | tf_op jit(solution)/shard_map/pallas_call | solution.py:235
  94.1 0.0 copy-start
  94.1 1.6 %copy.17 = bf16[128,384]{1,0:T(8,128)(2,1)} copy(bf16[128,384]{1,0:T(8,128)(2,1)} %get-tuple-element.12) | data formatting | bytes 196608
  95.7 1.6 %copy.18 = f32[128,384]{1,0:T(8,128)} copy(f32[128,384]{1,0:T(8,128)} %get-tuple-element.13) | data formatting | bytes 393216
  97.3 0.0 copy-done
  97.3 0.7 copy.19
Async XLA Ops:
  0.6 0.7 copy-start.1
  94.1 3.2 %copy-start = (bf16[512,384]{1,0:T(8,128)(2,1)S(1)}, bf16[512,384]{1,0:T(8,128)(2,1)}, u32[]{:S(2)}) copy-start(bf16[512,384]{1,0:T(8,128)(2,1)} %get-tuple-element.14) | copy-start | bytes 1179652

commit v8 on v7

--- a/solution.py
+++ b/solution.py
@@ -214,6 +214,26 @@
         hist_out[...] = (hist_out[...].astype(f32) - rstep_ref[...] * pulled).astype(bf16)
         if r == ROUNDS - 1:
             pulled_out[...] = pulled
+
+
+def hand_over_kernel(a_ref, b_ref, c_ref, a_out, b_out, c_out, sems):
+    copies = [pltpu.make_async_copy(src, dst, sems.at[i])
+              for i, (src, dst) in enumerate(((a_ref, a_out), (b_ref, b_out), (c_ref, c_out)))]
+    for cp in copies:
+        cp.start()
+    for cp in copies:
+        cp.wait()
+
+
+def hand_over(results):
+    anywhere = pl.BlockSpec(memory_space=pl.ANY)
+    return pl.pallas_call(
+        hand_over_kernel,
+        out_shape=tuple(jax.ShapeDtypeStruct(x.shape, x.dtype) for x in results),
+        in_specs=[anywhere] * 3,
+        out_specs=(anywhere,) * 3,
+        scratch_shapes=[pltpu.SemaphoreType.DMA((3,))],
+    )(*results)
 
 
 def shards(history, routes, dam_field, conn_free, conn_dam, stiff_ref, stiff_coef,
@@ -271,7 +291,7 @@
             collective_id=0, has_side_effects=True, vmem_limit_bytes=60 * 1024 * 1024),
     )(stiff_coef, mass_coef, history, dam_field, conn_free, conn_dam, stiff_ref,
       dam_step.reshape(1, -1), reg_step.reshape(1, -1), routes)
-    return (outs[0], outs[1], outs[2])
+    return hand_over((outs[0], outs[1], outs[2]))
 
 
 def solution(mesh):

time: 98.4 us -> 116 us (1.18)
  Pallas kernels: 92 us -> 114 us
  local copies, waits for them, and re-layouts: 5.37 us -> 1.41 us
    pallas_call x0 -> x1, Pallas kernels: none -> 22 us  [hand_over(): pl.pallas_call(hand_over_kernel, out_shape=tuple((jax.ShapeDtypeStruct(x....]
    unnamed x8 -> x3, local copies, waits for them, and re-layouts: 5.37 us -> 1.41 us
where the time goes in v8:
time: 116 us
  Pallas kernels  114 us (98%)
  local copies, waits for them, and re-layouts  1.41 us (1%)
    pallas_call x1, Pallas kernels, shards(): pl.pallas_call(functools.partial(coupling_kernel, devices, ndam), out_sha...  92 us
    pallas_call x1, Pallas kernels, hand_over(): pl.pallas_call(hand_over_kernel, out_shape=tuple((jax.ShapeDtypeStruct(x....  22 us

profile of v8, /device:TPU:1, one launch (start us, length us, event | category | flops | bytes accessed | tf_op | source)
XLA Modules:
  0.0 116.0 jit_solution(4091678967710259003)
XLA Ops:
  0.6 0.0 copy-start
  0.6 0.7 copy-done
  1.3 0.7 copy.13.routes_ref
  2.1 92.0 %shard_map.121 = (bf16[128,384]{1,0:T(8,128)(2,1)}, f32[128,384]{1,0:T(8,128)}, bf16[512,384]{1,0:T(8,128)(2,1)}, bf16[128,4,384]{2,1,0:T(4,128)(2,1)}, bf16[128...) custom-call(f32[64]{0:T(128)} %sc_ref.1, f32[64]{0:T(128)} %mc_ref.1, ...), custom_call_target="tpu_custom_call" | custom-call | tf_op jit(solution)/shard_map/pallas_call | solution.py:255
  94.1 22.0 %shard_map.122 = (bf16[128,384]{1,0:T(8,128)(2,1)}, f32[128,384]{1,0:T(8,128)}, bf16[512,384]{1,0:T(8,128)(2,1)}) custom-call(bf16[128,384]{1,0:T(8,128)(2,1)} %get-tuple-element.6.a_ref, f32[128,384]{1,0:T(8,128)} %get-tuple-element.7.b_ref, bf16[512,384]{1,0:T(8,128)(2,1)} %get-tuple-element.8.c_ref), custom_call_target="tpu_custom_call" | custom-call | tf_op jit(solution)/shard_map/pallas_call | solution.py:230
Async XLA Ops:
  0.6 0.7 copy-start

commit v9 on v7

--- a/solution.py
+++ b/solution.py
@@ -64,24 +64,24 @@
     pick_cols = (across == (down % nodes) * 3 + down // nodes).astype(bf16)
     permuted = jnp.dot(pick_rows, stiff_ref[...], preferred_element_type=f32).astype(bf16)
     sp_ref[...] = jnp.dot(permuted, pick_cols, preferred_element_type=f32).astype(bf16)
-    regional = routes_ref.shape[0]
+    regional = routes_ref.shape[1]
     capacity = slots // n
-    first = routes_ref[:, 0:1]
-    second = routes_ref[:, 1:2]
-    numbers = lax.broadcasted_iota(jnp.int32, (regional, n), 1)
+    first = routes_ref[0:1, :]
+    second = routes_ref[1:2, :]
+    numbers = lax.broadcasted_iota(jnp.int32, (n, regional), 0)
     hit_first = (first == numbers).astype(f32)
     hit_second = (second == numbers).astype(f32)
-    earlier = (lax.broadcasted_iota(jnp.int32, (regional, regional), 1)
-               < lax.broadcasted_iota(jnp.int32, (regional, regional), 0)).astype(bf16)
-    counts = jnp.dot(earlier, (hit_first + hit_second).astype(bf16), preferred_element_type=f32)
-    slot_first = jnp.sum(counts * hit_first, axis=1, keepdims=True).astype(jnp.int32)
-    slot_second = jnp.sum(counts * hit_second, axis=1, keepdims=True).astype(jnp.int32)
+    earlier = (lax.broadcasted_iota(jnp.int32, (regional, regional), 0)
+               < lax.broadcasted_iota(jnp.int32, (regional, regional), 1)).astype(bf16)
+    counts = jnp.dot((hit_first + hit_second).astype(bf16), earlier, preferred_element_type=f32)
+    slot_first = jnp.sum(counts * hit_first, axis=0, keepdims=True).astype(jnp.int32)
+    slot_second = jnp.sum(counts * hit_second, axis=0, keepdims=True).astype(jnp.int32)
     place_first = first * capacity + slot_first
     place_second = second * capacity + slot_second
-    columns = lax.broadcasted_iota(jnp.int32, (regional, slots), 1)
-    pair = jnp.logical_or(columns == place_first, columns == place_second).astype(f32)
-    q_ref[...] = pair.astype(bf16)
-    qt_ref[...] = jnp.transpose(pair).astype(bf16)
+    positions = lax.broadcasted_iota(jnp.int32, (slots, regional), 0)
+    pair = jnp.logical_or(positions == place_first, positions == place_second).astype(f32)
+    qt_ref[...] = pair.astype(bf16)
+    q_ref[...] = jnp.transpose(pair).astype(bf16)
     dstep_ref[...] = jnp.transpose(
         jnp.broadcast_to(dstep_row[...], (8, dstep_row.shape[1])))[:, 0:1]
     rstep_ref[...] = jnp.transpose(
@@ -270,7 +270,7 @@
         compiler_params=pltpu.CompilerParams(
             collective_id=0, has_side_effects=True, vmem_limit_bytes=60 * 1024 * 1024),
     )(stiff_coef, mass_coef, history, dam_field, conn_free, conn_dam, stiff_ref,
-      dam_step.reshape(1, -1), reg_step.reshape(1, -1), routes)
+      dam_step.reshape(1, -1), reg_step.reshape(1, -1), jnp.transpose(routes))
     return (outs[0], outs[1], outs[2])
 
 

time: 98.4 us -> 96.9 us (0.985)
  local copies, waits for them, and re-layouts: 5.37 us -> 3.96 us
    unnamed x8 -> x5, local copies, waits for them, and re-layouts: 5.37 us -> 3.96 us
where the time goes in v9:
time: 96.9 us; the launch traced here: 96.5 us
  Pallas kernels  91.9 us (95%)
  local copies, waits for them, and re-layouts  3.96 us (4%)
    pallas_call x1, Pallas kernels, shards(): pl.pallas_call(functools.partial(coupling_kernel, devices, ndam), out_sha...  91.9 us
    unnamed x5, local copies, waits for them, and re-layouts  3.96 us

profile of v9, /device:TPU:1, one launch (start us, length us, event | category | flops | bytes accessed | tf_op | source)
XLA Modules:
  0.0 96.5 jit_solution(4964083374047280421)
XLA Ops:
  0.6 91.9 %shard_map.121 = (bf16[128,384]{1,0:T(8,128)(2,1)}, f32[128,384]{1,0:T(8,128)}, bf16[512,384]{1,0:T(8,128)(2,1)}, bf16[128,4,384]{2,1,0:T(4,128)(2,1)}, bf16[128...) custom-call(f32[64]{0:T(128)} %sc_ref.1, f32[64]{0:T(128)} %mc_ref.1, ...), custom_call_target="tpu_custom_call" | custom-call | tf_op jit(solution)/shard_map/pallas_call | solution.py:235
  92.6 0.0 copy-start
  92.6 1.6 %copy.16 = bf16[128,384]{1,0:T(8,128)(2,1)} copy(bf16[128,384]{1,0:T(8,128)(2,1)} %get-tuple-element.12) | data formatting | bytes 196608
  94.2 1.6 %copy.17 = f32[128,384]{1,0:T(8,128)} copy(f32[128,384]{1,0:T(8,128)} %get-tuple-element.13) | data formatting | bytes 393216
  95.8 0.0 copy-done
  95.8 0.7 copy.18
Async XLA Ops:
  92.6 3.2 %copy-start = (bf16[512,384]{1,0:T(8,128)(2,1)S(1)}, bf16[512,384]{1,0:T(8,128)(2,1)}, u32[]{:S(2)}) copy-start(bf16[512,384]{1,0:T(8,128)(2,1)} %get-tuple-element.14) | copy-start | bytes 1179652

commit v10 on v9

--- a/solution.py
+++ b/solution.py
@@ -8,7 +8,7 @@
 from jax.sharding import PartitionSpec as P
 
 ROUNDS = 2
-GROUP = 4
+GROUP = 8
 GATHER_PARTS = 4
 
 

time: 96.9 us -> 92.2 us (0.951)
  Pallas kernels: 91.9 us -> 87.3 us
    pallas_call x1, Pallas kernels: 91.9 us -> 87.3 us  [shards(): pl.pallas_call(functools.partial(coupling_kernel, devices, ndam), out_sha...]
where the time goes in v10:
time: 92.2 us; the launch traced here: 91.9 us
  Pallas kernels  87.3 us (95%)
  local copies, waits for them, and re-layouts  3.96 us (4%)
    pallas_call x1, Pallas kernels, shards(): pl.pallas_call(functools.partial(coupling_kernel, devices, ndam), out_sha...  87.3 us
    unnamed x5, local copies, waits for them, and re-layouts  3.96 us

profile of v10, /device:TPU:1, one launch (start us, length us, event | category | flops | bytes accessed | tf_op | source)
XLA Modules:
  0.0 91.9 jit_solution(8474389793364970281)
XLA Ops:
  0.6 87.3 %shard_map.121 = (bf16[128,384]{1,0:T(8,128)(2,1)}, f32[128,384]{1,0:T(8,128)}, bf16[512,384]{1,0:T(8,128)(2,1)}, bf16[128,4,384]{2,1,0:T(4,128)(2,1)}, bf16[128...) custom-call(f32[64]{0:T(128)} %sc_ref.1, f32[64]{0:T(128)} %mc_ref.1, ...), custom_call_target="tpu_custom_call" | custom-call | tf_op jit(solution)/shard_map/pallas_call | solution.py:235
  87.9 0.0 copy-start
  87.9 1.6 %copy.16 = bf16[128,384]{1,0:T(8,128)(2,1)} copy(bf16[128,384]{1,0:T(8,128)(2,1)} %get-tuple-element.12) | data formatting | bytes 196608
  89.5 1.6 %copy.17 = f32[128,384]{1,0:T(8,128)} copy(f32[128,384]{1,0:T(8,128)} %get-tuple-element.13) | data formatting | bytes 393216
  91.1 0.0 copy-done
  91.1 0.7 copy.18
Async XLA Ops:
  87.9 3.2 %copy-start = (bf16[512,384]{1,0:T(8,128)(2,1)S(1)}, bf16[512,384]{1,0:T(8,128)(2,1)}, u32[]{:S(2)}) copy-start(bf16[512,384]{1,0:T(8,128)(2,1)} %get-tuple-element.14) | copy-start | bytes 1179652

commit v11 on v10

--- a/solution.py
+++ b/solution.py
@@ -8,7 +8,7 @@
 from jax.sharding import PartitionSpec as P
 
 ROUNDS = 2
-GROUP = 8
+GROUP = 16
 GATHER_PARTS = 4
 
 

time: 92.2 us -> 89.7 us (0.973)
  Pallas kernels: 87.3 us -> 84.8 us
    pallas_call x1, Pallas kernels: 87.3 us -> 84.8 us  [shards(): pl.pallas_call(functools.partial(coupling_kernel, devices, ndam), out_sha...]
where the time goes in v11:
time: 89.7 us; the launch traced here: 89.4 us
  Pallas kernels  84.8 us (95%)
  local copies, waits for them, and re-layouts  3.96 us (4%)
    pallas_call x1, Pallas kernels, shards(): pl.pallas_call(functools.partial(coupling_kernel, devices, ndam), out_sha...  84.8 us
    unnamed x5, local copies, waits for them, and re-layouts  3.96 us

profile of v11, /device:TPU:1, one launch (start us, length us, event | category | flops | bytes accessed | tf_op | source)
XLA Modules:
  0.0 89.4 jit_solution(3338490012867521799)
XLA Ops:
  0.6 84.8 %shard_map.121 = (bf16[128,384]{1,0:T(8,128)(2,1)}, f32[128,384]{1,0:T(8,128)}, bf16[512,384]{1,0:T(8,128)(2,1)}, bf16[128,4,384]{2,1,0:T(4,128)(2,1)}, bf16[128...) custom-call(f32[64]{0:T(128)} %sc_ref.1, f32[64]{0:T(128)} %mc_ref.1, ...), custom_call_target="tpu_custom_call" | custom-call | tf_op jit(solution)/shard_map/pallas_call | solution.py:235
  85.4 0.0 copy-start
  85.4 1.6 %copy.16 = bf16[128,384]{1,0:T(8,128)(2,1)} copy(bf16[128,384]{1,0:T(8,128)(2,1)} %get-tuple-element.12) | data formatting | bytes 196608
  87.0 1.6 %copy.17 = f32[128,384]{1,0:T(8,128)} copy(f32[128,384]{1,0:T(8,128)} %get-tuple-element.13) | data formatting | bytes 393216
  88.6 0.0 copy-done
  88.6 0.7 copy.18
Async XLA Ops:
  85.4 3.2 %copy-start = (bf16[512,384]{1,0:T(8,128)(2,1)S(1)}, bf16[512,384]{1,0:T(8,128)(2,1)}, u32[]{:S(2)}) copy-start(bf16[512,384]{1,0:T(8,128)(2,1)} %get-tuple-element.14) | copy-start | bytes 1179652

commit v12 on v11

--- a/solution.py
+++ b/solution.py
@@ -8,7 +8,7 @@
 from jax.sharding import PartitionSpec as P
 
 ROUNDS = 2
-GROUP = 16
+GROUP = 32
 GATHER_PARTS = 4
 
 

time: 89.7 us -> 88.5 us (0.987)
  Pallas kernels: 84.8 us -> 83.5 us
    pallas_call x1, Pallas kernels: 84.8 us -> 83.5 us  [shards(): pl.pallas_call(functools.partial(coupling_kernel, devices, ndam), out_sha...]
where the time goes in v12:
time: 88.5 us; the launch traced here: 88.1 us
  Pallas kernels  83.5 us (94%)
  local copies, waits for them, and re-layouts  3.96 us (4%)
    pallas_call x1, Pallas kernels, shards(): pl.pallas_call(functools.partial(coupling_kernel, devices, ndam), out_sha...  83.5 us
    unnamed x5, local copies, waits for them, and re-layouts  3.96 us

profile of v12, /device:TPU:1, one launch (start us, length us, event | category | flops | bytes accessed | tf_op | source)
XLA Modules:
  0.0 88.1 jit_solution(10119641196440115540)
XLA Ops:
  0.6 83.5 %shard_map.121 = (bf16[128,384]{1,0:T(8,128)(2,1)}, f32[128,384]{1,0:T(8,128)}, bf16[512,384]{1,0:T(8,128)(2,1)}, bf16[128,4,384]{2,1,0:T(4,128)(2,1)}, bf16[128...) custom-call(f32[64]{0:T(128)} %sc_ref.1, f32[64]{0:T(128)} %mc_ref.1, ...), custom_call_target="tpu_custom_call" | custom-call | tf_op jit(solution)/shard_map/pallas_call | solution.py:235
  84.2 0.0 copy-start
  84.2 1.6 %copy.16 = bf16[128,384]{1,0:T(8,128)(2,1)} copy(bf16[128,384]{1,0:T(8,128)(2,1)} %get-tuple-element.12) | data formatting | bytes 196608
  85.8 1.6 %copy.17 = f32[128,384]{1,0:T(8,128)} copy(f32[128,384]{1,0:T(8,128)} %get-tuple-element.13) | data formatting | bytes 393216
  87.4 0.0 copy-done
  87.4 0.7 copy.18
Async XLA Ops:
  84.2 3.2 %copy-start = (bf16[512,384]{1,0:T(8,128)(2,1)S(1)}, bf16[512,384]{1,0:T(8,128)(2,1)}, u32[]{:S(2)}) copy-start(bf16[512,384]{1,0:T(8,128)(2,1)} %get-tuple-element.14) | copy-start | bytes 1179652
